TPU v7x, 32 devices: a whole 2x2x4 slice. The times are simulated.
32 devices in a mesh: dp: 4 (over x, core), ctx: 8 (over z, y).
Axes of the slice: x: 2, y: 2, z: 4, core: 2. Of those that a mesh axis runs over, the one named last changes fastest.
Arguments:
- hidden_in: bfloat16 [4, 1024, 960], P('dp', 'ctx'), may hold values from -6 to 6
- positions: int32 [4, 1024], P('dp', 'ctx'), may hold values from 0 to 1023, as said below
- attn_gain: bfloat16 [960], P('ctx'), may hold values from 0.099609375 to 1.8984375
- query_w: bfloat16 [960, 960], P('ctx', 'dp'), may hold values from -0.1875 to 0.1875
- key_w: bfloat16 [960, 320], P('ctx', 'dp'), may hold values from -0.1875 to 0.1875
- value_weight: bfloat16 [960, 320], P('ctx', 'dp'), may hold values from -0.1875 to 0.1875
- output_weight: bfloat16 [960, 960], P('ctx', 'dp'), may hold values from -3.5 to 3.5
- ffn_gain: bfloat16 [960], P('ctx'), may hold values from 0.099609375 to 1.8984375
- gate_w: bfloat16 [960, 2560], P('ctx', 'dp'), may hold values from -0.1875 to 0.1875
- up_w: bfloat16 [960, 2560], P('ctx', 'dp'), may hold values from -0.1875 to 0.1875
- down_w: bfloat16 [2560, 960], P('ctx', 'dp'), may hold values from -0.125 to 0.125
- cotangent: bfloat16 [4, 1024, 960], P('dp', 'ctx'), may hold values from -6 to 6
Outputs:
- hidden_out: float32 [4, 1024, 960], P('dp', 'ctx')
- grad_in: float32 [4, 1024, 960], P('dp', 'ctx')
- grad_attn_gain: float32 [960], P('ctx')
- grad_query: float32 [960, 960], P('ctx', 'dp')
- grad_key: float32 [960, 320], P('ctx', 'dp')
- grad_value: float32 [960, 320], P('ctx', 'dp')
- grad_out: float32 [960, 960], P('ctx', 'dp')
- grad_ffn_gain: float32 [960], P('ctx')
- grad_gate: float32 [960, 2560], P('ctx', 'dp')
- grad_up: float32 [960, 2560], P('ctx', 'dp')
- grad_down: float32 [2560, 960], P('ctx', 'dp')
Inputs may be any that keep to these rules, and one draw needn't show every extreme that they name: In each sequence every position 0 to 1023 appears once. The 128 tokens of ctx shard c of a sequence are two aligned blocks: positions j * 64 onward and then (15 - j) * 64 onward, for a pair number j that is a permutation of the shards, drawn afresh for each sequence.
All inputs are finite; a program needn't handle non-finite values.
Results may differ from a plain program's by a relative error of at most 0.014.
Values may be sent and summed in bfloat16 or wider, within the bound.
No kernel may reach another device: no remote copies, remote signals or barrier semaphores. Data moves between devices by JAX's collectives and lax.ppermute only.
A program may use at most 192 MiB of HBM per device.

v0:
```python
import functools
from types import SimpleNamespace

import jax
import jax.numpy as jnp
from jax import lax
from jax.experimental import pallas as pl
from jax.experimental.pallas import tpu as pltpu
from jax.sharding import PartitionSpec as P


QH = 15
KVH = 5
HD = 64
HALF = HD // 2
GRP = QH // KVH
KVW = KVH * HD
eps = 1e-05
rope_base = 10000.0
neg_big = -1e30
AX = ("dp", "ctx")
f32 = jnp.float32
bf16 = jnp.bfloat16


SLOTS = ((0, 0), (1, 0), (0, 1), (1, 1))


def moved(z, x, target):
    table = []
    for d in range(z.nd):
        for c in range(z.nc):
            dd, cc = target(d, c)
            table.append((d * z.nc + c, dd * z.nc + cc))
    return lax.ppermute(x, AX, table)


def to_slot(z, x, i):
    fx, fy = SLOTS[i]
    return moved(z, x, lambda d, c: (d ^ (2 * fx), c ^ fy))


def to_core(z, x):
    return moved(z, x, lambda d, c: (d ^ 1, c))


def from_line(z, x, k):
    return moved(z, x, lambda d, c: (d, 2 * ((c // 2 - k) % z.length) + c % 2))


def inner(z, x, toward_middle, outward):
    table = []
    for d in range(z.nd):
        for c in range(z.nc):
            l = c // 2
            to = {1: 2, 2: 1} if not outward else {1: 0, 2: 3}
            if outward and toward_middle:
                to = {0: 1, 3: 2}
            if l in to:
                table.append((d * z.nc + c, d * z.nc + 2 * to[l] + c % 2))
    return lax.ppermute(x, AX, table)


def line_pieces(z, x):
    L = z.length
    if L != 4:
        return [x] + [from_line(z, x, k) for k in range(1, L)]
    one, three = from_line(z, x, 1), from_line(z, x, 3)
    l = lax.axis_index("ctx") // 2
    out = jnp.where(l == 1, one, three)
    across = jnp.where(l == 1, three, one)
    p = inner(z, out, False, True)
    q = inner(z, across, False, False)
    return [x, one, jnp.where((l == 0) | (l == 3), p, q), three]


def nt(a, b):
    return lax.dot_general(a, b, (((1,), (1,)), ((), ())), preferred_element_type=f32)


def nn(a, b):
    return lax.dot_general(a, b, (((1,), (0,)), ((), ())), preferred_element_type=f32)


def tn(a, b):
    return lax.dot_general(a, b, (((0,), (0,)), ((), ())), preferred_element_type=f32)


def place():
    d0, c0 = lax.axis_index("dp"), lax.axis_index("ctx")
    return SimpleNamespace(x=d0 // 2, core=lax.rem(d0, 2), l=c0 // 2, y=lax.rem(c0, 2))


def flip(bit, f):
    return 1 - bit if f else bit


def d_of(at, fx, fcore):
    return 2 * flip(at.x, fx) + flip(at.core, fcore)


def c_of(z, at, fy, k):
    return 2 * lax.rem(at.l + k, z.length) + flip(at.y, fy)


def pieces_of(pieces, fy):
    return [(pieces[4 * fcore + fx + 2 * fy], fx, fcore) for fcore in (0, 1) for fx in (0, 1)]


def gathered(z, at, ref, fy):
    return jnp.concatenate([ref[c_of(z, at, fy, k)] for k in range(z.length)], axis=0)


def seen(z, at, k):
    return lax.rem(at.l + k, z.nd) if z.fold == 1 else k


VM = pl.BlockSpec(memory_space=pltpu.VMEM)


def call(kernel, z, outs, args, scratch=(), flops=0):
    moved_bytes = sum(a.size * a.dtype.itemsize for a in args)
    moved_bytes += sum(o.size * o.dtype.itemsize for o in outs)
    return pl.pallas_call(
        functools.partial(kernel, z),
        out_shape=tuple(outs),
        in_specs=[VM] * len(args),
        out_specs=tuple([VM] * len(outs)),
        scratch_shapes=list(scratch),
        compiler_params=pltpu.CompilerParams(vmem_limit_bytes=56 << 20),
        cost_estimate=pl.CostEstimate(
            flops=int(flops), transcendentals=0, bytes_accessed=int(moved_bytes)
        ),
    )(*args)


def sds(shape, dtype):
    return jax.ShapeDtypeStruct(shape, dtype)


def rotate(rows, cos, sin):
    out = []
    for i in range(rows.shape[0] // HD):
        a, b = rows[HD * i : HD * i + HALF], rows[HD * i + HALF : HD * (i + 1)]
        out += [a * cos - b * sin, b * cos + a * sin]
    return jnp.concatenate(out, axis=0)


def first_kernel(z, key_ref, value_ref, gain_one_ref, gain_two_ref, places_ref, out_ref):
    half = z.tokens // 2
    blocks = [places_ref[0:1, half * i : half * i + 1].astype(f32) * (1.0 / half) for i in (0, 1)]
    rows = [gain_one_ref[...].astype(f32), gain_two_ref[...].astype(f32)]
    rows += [jnp.broadcast_to(b, (1, z.rows)) for b in blocks]
    rows += [jnp.zeros((4, z.rows), f32)]
    out_ref[: z.kw] = key_ref[...]
    out_ref[z.kw : 2 * z.kw] = value_ref[...]
    out_ref[2 * z.kw :] = jnp.concatenate(rows, axis=0).astype(bf16)


def first_call(z, key, value, gain_one, gain_two, places):
    outs = [sds((2 * z.kw + 8, z.rows), bf16)]
    args = [key, value, gain_one[None], gain_two[None], places]
    return call(first_kernel, z, outs, args)[0]


def kv_kernel(z, x_ref, cos_ref, sin_ref, *refs):
    pieces, (kv_ref, n1_ref, inv_ref, gain_ref, small_ref, acc_ref, sum_ref) = refs[:8], refs[8:]
    at = place()
    x = x_ref[...].astype(f32)
    mean = jnp.sum(jnp.sum(x * x, axis=0), axis=0, keepdims=True) * (1.0 / z.width)
    inv = lax.rsqrt(mean + eps)
    inv_ref[...] = jnp.broadcast_to(inv, inv_ref.shape)
    w = 2 * z.kw
    for fy, n in ((0, 0), (1, 2)):
        blocks = []
        for k in range(z.length):
            c = c_of(z, at, fy, k)
            small = pieces[n][k, w : w + 8, :].astype(f32)
            small_ref[c] = small
            gain = jnp.transpose(small)
            gain_ref[c] = gain
            block = x_ref[c].astype(f32) * inv * gain[:, 0:1]
            blocks.append(block)
            weights = jnp.concatenate([p[k, :w, :] for p, _, _ in pieces_of(pieces, fy)], axis=0)
            out = nn(weights, block.astype(bf16))
            if fy == 0 and k == 0:
                sum_ref[...] = out
            else:
                sum_ref[...] += out
        n1_ref[fy] = jnp.concatenate(blocks, axis=0).astype(bf16)
    for i, (_, fx, fcore) in enumerate(pieces_of(pieces, 0)):
        acc_ref[d_of(at, fx, fcore)] = sum_ref[w * i : w * (i + 1)]
    key = jnp.concatenate([acc_ref[d, : z.kw] for d in range(z.nd)], axis=0)
    value = jnp.concatenate([acc_ref[d, z.kw :] for d in range(z.nd)], axis=0)
    kv_ref[:KVW] = rotate(key, cos_ref[...], sin_ref[...]).astype(bf16)
    kv_ref[KVW:] = value.astype(bf16)


def kv_call(z, x_c, cos, sin, pieces):
    t = z.tokens
    outs = [
        sds((2 * KVW, t), bf16),
        sds((2, z.length * z.rows, t), bf16),
        sds((8, t), f32),
        sds((z.nc, z.rows, 8), f32),
        sds((z.nc, 8, z.rows), f32),
    ]
    scratch = [pltpu.VMEM((z.nd, 2 * z.kw, t), f32), pltpu.VMEM((z.nd * 2 * z.kw, t), f32)]
    return call(kv_kernel, z, outs, [x_c, cos, sin] + pieces, scratch, 2 * t * z.width * 2 * KVW)


def q_kernel(z, n1_ref, cos_ref, sin_ref, *refs):
    pieces, (q_ref, acc_ref) = refs[:8], refs[8:]
    at = place()
    for (low, fx, fcore), (high, _, _) in zip(pieces_of(pieces, 0), pieces_of(pieces, 1)):
        out = tn(low[:, : z.qw], n1_ref[0]) + tn(high[:, : z.qw], n1_ref[1])
        acc_ref[d_of(at, fx, fcore)] = out
    q = jnp.concatenate([acc_ref[d] for d in range(z.nd)], axis=0)
    q_ref[...] = rotate(q, cos_ref[...], sin_ref[...]).astype(bf16)


def q_call(z, n1, cos, sin, pieces):
    scratch = [pltpu.VMEM((z.nd, z.qw, z.tokens), f32)]
    outs = [sds((QH * HD, z.tokens), bf16)]
    return call(q_kernel, z, outs, [n1, cos, sin] + pieces, scratch, 2 * z.tokens * z.width**2)[0]


def lay_keys(z, at, chunks, small_ref, places_ref, kv_ref, bias_ref):
    t = z.tokens
    row = lax.broadcasted_iota(jnp.int32, (t, t), 0)
    low = row < t // 2
    within = jnp.where(low, row, row - t // 2).astype(f32)
    places = places_ref[0:1, :]
    for n, chunk in enumerate(chunks):
        kv_ref[:, t * n : t * (n + 1)] = chunk[...]
        c = c_of(z, at, n // z.length, n % z.length)
        small = small_ref[c]
        start = jnp.where(low, small[2:3, 0:1], small[3:4, 0:1]) * float(t // 2)
        bias_ref[t * n : t * (n + 1), :] = jnp.where(start + within <= places, 0.0, neg_big)


def three(ref, h):
    return jnp.concatenate([head_of(ref, GRP * h + g) for g in range(GRP)], axis=1)


def scores(kv_ref, bias_ref, h, q3):
    s = tn(head_of(kv_ref, h), q3) * (HD**-0.5)
    bias = bias_ref[...]
    return s + jnp.concatenate([bias] * GRP, axis=1)


def each_head(z, body):
    if z.nc <= 8:
        for h in range(KVH):
            body(h)
    else:
        lax.fori_loop(0, KVH, lambda h, carry: (body(h), carry)[1], 0)


def head_of(ref, n):
    start = HD * n
    return ref[pl.ds(start if isinstance(n, int) else pl.multiple_of(start, HD), HD), :]


def put_head(ref, n, x):
    start = HD * n
    ref[pl.ds(start if isinstance(n, int) else pl.multiple_of(start, HD), HD), :] = x


def forward_kernel(z, small_ref, places_ref, q_ref, x_ref, gain_ref, *refs):
    n = z.nc
    chunks, pieces = refs[:n], refs[n : n + 8]
    mix_ref, rows_out_ref, lse_ref, mid_ref, inv_ref, n2_ref = refs[n + 8 : n + 14]
    kv_ref, bias_ref, rows_ref, block_ref = refs[n + 14 :]
    at = place()
    t = z.tokens
    lay_keys(z, at, chunks, small_ref, places_ref, kv_ref, bias_ref)

    def head(h):
        s = scores(kv_ref, bias_ref, h, three(q_ref, h))
        top = jnp.max(s, axis=0, keepdims=True)
        e = jnp.exp(s - top)
        total = jnp.sum(e, axis=0, keepdims=True)
        lse_ref[pl.ds(h, 1), :] = top + jnp.log(total)
        p = (e * (1.0 / total)).astype(bf16)
        out = nn(head_of(kv_ref, KVH + h), p)
        for g in range(GRP):
            put_head(rows_ref, GRP * h + g, out[:, t * g : t * (g + 1)])

    each_head(z, head)
    mix = rows_ref[...]
    rows_out_ref[...] = mix.astype(bf16)
    for c in range(z.nc):
        block_ref[c] = mix[z.rows * c : z.rows * (c + 1)]
    for fy in (0, 1):
        mix_ref[fy] = gathered(z, at, block_ref, fy).astype(bf16)
    square = jnp.zeros((1, t), f32)
    part = slice(z.lane, z.lane + z.qw)
    for (low, fx, fcore), (high, _, _) in zip(pieces_of(pieces, 0), pieces_of(pieces, 1)):
        d = d_of(at, fx, fcore)
        mid = x_ref[d].astype(f32) + tn(low[:, part], mix_ref[0]) + tn(high[:, part], mix_ref[1])
        mid_ref[d] = mid
        square = square + jnp.sum(mid * mid, axis=0, keepdims=True)
    inv = lax.rsqrt(square * (1.0 / z.width) + eps)
    inv_ref[...] = jnp.broadcast_to(inv, inv_ref.shape)
    for k in range(z.nd):
        d = seen(z, at, k)
        n2_ref[k] = (mid_ref[d] * inv * gain_ref[d][:, 1:2]).astype(bf16)


def forward_call(z, small, places, q, x_d, gain_d, chunks, pieces):
    t = z.tokens
    outs = [
        sds((2, z.length * z.rows, t), bf16),
        sds((QH * HD, t), bf16),
        sds((8, GRP * t), f32),
        sds((z.nd, z.qw, t), f32),
        sds((8, t), f32),
        sds((z.nd, z.qw, t), bf16),
    ]
    scratch = [
        pltpu.VMEM((2 * KVW, z.nc * t), bf16),
        pltpu.VMEM((z.nc * t, t), f32),
        pltpu.VMEM((QH * HD, t), f32),
        pltpu.VMEM((z.nc, z.rows, t), f32),
    ]
    args = [small, places, q, x_d, gain_d] + chunks + pieces
    flops = 4 * z.nc * t * t * QH * HD + 2 * t * z.width**2
    return call(forward_kernel, z, outs, args, scratch, flops)


def ffn_act(z, gate, up, act_grad, act_ref, gu_ref):
    u = z.units
    sigma = jax.nn.sigmoid(gate)
    gs = gate * sigma
    act_ref[...] = (gs * up).astype(bf16)
    gu_ref[:u] = (act_grad * up * sigma * (1.0 + gate * (1.0 - sigma))).astype(bf16)
    gu_ref[u:] = (act_grad * gs).astype(bf16)


def give_slots(z, out, d, mine_ref, other_ref):
    t = z.tokens
    for i in range(4):
        mine_ref[i, d] = out[:, t * i : t * (i + 1)].astype(bf16)
        other_ref[i, d] = out[:, t * (4 + i) : t * (5 + i)].astype(bf16)


KEPT = (0, 1, 3, 2)


def ffn_first_kernel(z, *refs):
    t, u, b = z.tokens, z.units, 2 * z.rows
    cots, ws = refs[:8], refs[8:11]
    w_ref, turned_ref, cot_ref, grad_ref = refs[11:]
    at = place()
    for n, k in enumerate(KEPT):
        if n < 3:
            w_ref[b * n : b * (n + 1), :] = ws[n][...]
        for i in range(8):
            cot_ref[b * n : b * (n + 1), t * i : t * (i + 1)] = cots[i][seen(z, at, k)]
    turned_ref[...] = jnp.transpose(w_ref[:, : 2 * u])
    grad_ref[...] = tn(w_ref[:, 2 * u :], cot_ref[: 3 * b, :])


def ffn_kernel(z, w_ref, turned_ref, grad_ref, cot_ref, far_ref, *refs):
    n2s, (mine_ref, other_ref, gu_ref, act_ref, n2_ref) = refs[:8], refs[8:]
    t, u, b = z.tokens, z.units, 2 * z.rows
    at = place()
    for n, k in enumerate(KEPT):
        for i in range(8):
            n2_ref[b * n : b * (n + 1), t * i : t * (i + 1)] = n2s[i][b * k : b * (k + 1), :]
    gate_up = nn(turned_ref[...], n2_ref[: 3 * b, :]) + tn(far_ref[:, : 2 * u], n2_ref[3 * b :, :])
    act_grad = grad_ref[...] + tn(far_ref[:, 2 * u :], cot_ref[3 * b :, :])
    ffn_act(z, gate_up[:u], gate_up[u:], act_grad, act_ref, gu_ref)
    for n, k in enumerate(KEPT):
        w = far_ref[:, : 2 * u] if n == 3 else w_ref[b * n : b * (n + 1), : 2 * u]
        give_slots(z, nn(w, gu_ref[...]), seen(z, at, k), mine_ref, other_ref)


def ffn_blocks_kernel(z, *refs):
    L = z.length
    n2s, cots, gus, dts = refs[:8], refs[8:16], refs[16 : 16 + L], refs[16 + L : 16 + 2 * L]
    mine_ref, other_ref, gu_ref, act_ref, n2_ref, cot_ref, pre_ref, ag_ref, line_ref, part_ref = refs[16 + 2 * L :]
    at = place()
    u, rows = z.units, 2 * z.rows
    t = z.tokens
    for i in range(8):
        n2_ref[:, t * i : t * (i + 1)] = n2s[i][...]
        for d in range(z.nd):
            part_ref[d, :, t * i : t * (i + 1)] = cots[i][d]
            cot_ref[z.qw * d : z.qw * (d + 1), t * i : t * (i + 1)] = cots[i][d]
    for l in range(L):
        line_ref[l] = n2_ref[rows * l : rows * (l + 1), :]
    pre_ref[...] = jnp.zeros_like(pre_ref)
    ag_ref[...] = jnp.zeros_like(ag_ref)
    for k in range(L):
        l = lax.rem(at.l + k, L)
        part, units = down_part(z, l)
        pre_ref[...] += tn(gus[k][...], line_ref[l])
        ag_ref[units, :] += tn(dts[k][...], part_ref[part])
    ffn_act(z, pre_ref[:u], pre_ref[u:], ag_ref[...], act_ref, gu_ref)
    for k in range(L):
        line_ref[lax.rem(at.l + k, L)] = nn(gus[k][...], gu_ref[...]).astype(bf16)
    for d in range(z.nd):
        out = jnp.concatenate([line_ref[z.fold * d + i] for i in range(z.fold)], axis=0)
        give_slots(z, out, d, mine_ref, other_ref)


def ffn_call(z, n2s, cots, gus, dts):
    t, L, u = z.tokens, z.length, z.units
    outs = [
        sds((4, z.nd, z.qw, t), bf16),
        sds((4, z.nd, z.qw, t), bf16),
        sds((2 * u, 8 * t), bf16),
        sds((u, 8 * t), bf16),
        sds((z.width, 8 * t), bf16),
        sds((z.width, 8 * t), bf16),
    ]
    flops = 2 * 8 * t * z.width * 5 * u
    if z.fold == 1:
        firsts = [
            sds((6 * z.rows, 3 * u), bf16),
            sds((2 * u, 6 * z.rows), bf16),
            outs[5],
            sds((u, 8 * t), f32),
        ]
        near = [gus[k] for k in KEPT[:3]]
        w, turned, cot, grad = call(ffn_first_kernel, z, firsts, cots + near, (), flops // 5)
        args = [w, turned, grad, cot, gus[KEPT[3]]] + n2s
        return list(call(ffn_kernel, z, outs[:5], args, (), flops)) + [cot]
    scratch = [
        pltpu.VMEM((2 * u, 8 * t), f32),
        pltpu.VMEM((u, 8 * t), f32),
        pltpu.VMEM((L, 2 * z.rows, 8 * t), bf16),
        pltpu.VMEM((z.nd, z.qw, 8 * t), bf16),
    ]
    return call(ffn_blocks_kernel, z, outs, n2s + cots + gus + dts, scratch, flops)


def down_part(z, l):
    i = lax.rem(l, z.fold)
    rows = slice(None) if z.fold == 1 else pl.ds(pl.multiple_of(i * z.down_rows, z.down_rows), z.down_rows)
    return l // z.fold, rows


def hidden_kernel(z, act_ref, *refs):
    L, u = z.length, z.units
    dts, (mine_ref, other_ref, sum_ref) = refs[:L], refs[L:]
    at = place()
    if z.fold == 1:
        for k in range(L):
            give_slots(z, nn(dts[k][:, 2 * u :], act_ref[...]), seen(z, at, k), mine_ref, other_ref)
    else:
        sum_ref[...] = jnp.zeros_like(sum_ref)
        for k in range(L):
            part, units = down_part(z, lax.rem(at.l + k, L))
            sum_ref[part] += nn(dts[k][...], act_ref[units, :])
        for d in range(z.nd):
            give_slots(z, sum_ref[d], d, mine_ref, other_ref)


def hidden_call(z, act, dts):
    t = z.tokens
    outs = [sds((4, z.nd, z.qw, t), bf16)] * 2
    scratch = [pltpu.VMEM((z.nd, z.qw, 8 * t) if z.fold != 1 else (8, 128), f32)]
    return call(hidden_kernel, z, outs, [act] + dts, scratch, 16 * t * z.width * z.units)


def ffn_weights_kernel(z, gu_ref, act_ref, n2_ref, cot_ref, *refs):
    L, u = z.length, z.units
    at = place()
    for n in range(L):
        k = KEPT[n] if z.fold == 1 else n
        rows = slice(2 * z.rows * n, 2 * z.rows * (n + 1))
        if z.fold == 1:
            refs[k][:, : 2 * u] = nt(n2_ref[rows, :], gu_ref[...]).astype(bf16)
            refs[k][:, 2 * u :] = nt(cot_ref[rows, :], act_ref[...]).astype(bf16)
        else:
            refs[2 * L][k] = nt(n2_ref[rows, :], gu_ref[...]).astype(bf16)
    if z.fold != 1:
        for d in range(z.nd):
            down = nt(cot_ref[z.qw * d : z.qw * (d + 1), :], act_ref[...])
            for i in range(z.fold):
                block = down[:, z.down_rows * i : z.down_rows * (i + 1)]
                refs[2 * L + 1][z.fold * d + i] = block.astype(bf16)
        for k in range(L):
            l = lax.rem(at.l + k, L)
            refs[k][...] = refs[2 * L][l]
            refs[L + k][...] = refs[2 * L + 1][l]


def ffn_weights_call(z, gu, act, n2, cot):
    L, scratch = z.length, []
    if z.fold == 1:
        outs = [sds((2 * z.rows, 3 * z.units), bf16)] * L
    else:
        shapes = (2 * z.rows, 2 * z.units), (z.qw, z.down_rows)
        outs = [sds(shape, bf16) for shape in shapes for _ in range(L)]
        scratch = [pltpu.VMEM((L,) + shape, bf16) for shape in shapes]
    flops = 2 * 8 * z.tokens * z.width * 3 * z.units
    out = call(ffn_weights_kernel, z, outs, [gu, act, n2, cot], scratch, flops)
    return out[:L], out[L:]


def core_sum(mine, got):
    total = [mine[i].astype(f32) + got[i].astype(f32) for i in range(4)]
    return [total[0]] + [part.astype(bf16) for part in total[1:]]


def slab_sum(z, own, got):
    out = []
    for k in range(z.length):
        n = own.shape[0] // z.length
        part = k if own.ndim == 3 else slice(n * k, n * (k + 1))
        total = own[part]
        for g in got:
            total = total + g[part].astype(f32)
        out.append(total if k == 0 else total.astype(bf16))
    return out


def backward_kernel(z, small_ref, places_ref, q_ref, mid_ref, inv_ref, gain_ref, cot_ref, mix_ref, lse_ref, cos_ref, sin_ref, own_ref, *refs):
    n = z.nc
    got, refs = refs[:3], refs[3:]
    chunks, pieces = refs[:n], refs[n : n + 8]
    midg_ref, midb_ref, gain_two_ref, dq_ref, *dkv_refs = refs[n + 8 : 2 * n + 12]
    kv_ref, bias_ref, grad_ref, dk_ref, rows_ref, dq_rows_ref = refs[2 * n + 12 :]
    at = place()
    t = z.tokens
    inv = inv_ref[0:1, :]
    mean = jnp.zeros((1, t), f32)
    for d in range(z.nd):
        g = own_ref[d] + got[0][d].astype(f32) + got[1][d].astype(f32) + got[2][d].astype(f32)
        mid = mid_ref[d]
        gain_two_ref[d] = jnp.broadcast_to(jnp.sum(g * mid * inv, axis=1, keepdims=True), (z.qw, 8))
        u = g * gain_ref[d][:, 1:2]
        midg_ref[d] = u
        mean = mean + jnp.sum(u * mid, axis=0, keepdims=True)
    scale = inv * inv * mean * (1.0 / z.width)
    for d in range(z.nd):
        full = cot_ref[d].astype(f32) + inv * (midg_ref[d] - mid_ref[d] * scale)
        midg_ref[d] = full
        midb_ref[d] = full.astype(bf16)
    part = slice(z.lane, z.lane + z.qw)
    for fy in (0, 1):
        acc = jnp.zeros((z.length * z.rows, t), f32)
        for piece, fx, fcore in pieces_of(pieces, fy):
            acc = acc + nn(piece[:, part], midb_ref[d_of(at, fx, fcore)])
        for k in range(z.length):
            grad_ref[c_of(z, at, fy, k)] = acc[z.rows * k : z.rows * (k + 1)]
    lay_keys(z, at, chunks, small_ref, places_ref, kv_ref, bias_ref)
    rows_ref[...] = jnp.concatenate([grad_ref[c] for c in range(z.nc)], axis=0)
    cos, sin = cos_ref[...], sin_ref[...]
    factor = HD**-0.5

    def head(h):
        q3 = three(q_ref, h)
        g3 = three(rows_ref, h).astype(bf16)
        delta = jnp.sum(g3.astype(f32) * three(mix_ref, h).astype(f32), axis=0, keepdims=True)
        key, value = head_of(kv_ref, h), head_of(kv_ref, KVH + h)
        p = jnp.exp(scores(kv_ref, bias_ref, h, q3) - lse_ref[pl.ds(h, 1), :])
        dv = nt(g3, p.astype(bf16))
        ds = (p * (tn(value, g3) - delta)).astype(bf16)
        dk = nt(q3, ds) * factor
        dq = nn(key, ds) * factor
        put_head(dk_ref, h, dk.astype(bf16))
        put_head(dk_ref, KVH + h, dv.astype(bf16))
        for g in range(GRP):
            put_head(dq_rows_ref, GRP * h + g, dq[:, t * g : t * (g + 1)])

    each_head(z, head)
    rows = rotate(dq_rows_ref[...], cos, -sin)
    for d in range(z.nd):
        dq_ref[d] = rows[z.qw * d : z.qw * (d + 1)].astype(bf16)
    for i, out in enumerate(dkv_refs):
        out[...] = dk_ref[:, t * i : t * (i + 1)]


def backward_call(z, small, places, q, mid, inv, gain_d, cot_d, mix, lse, cos, sin, own, got, chunks, pieces):
    t = z.tokens
    outs = [
        sds((z.nd, z.qw, t), f32),
        sds((z.nd, z.qw, t), bf16),
        sds((z.nd, z.qw, 8), f32),
        sds((z.nd, z.qw, t), bf16),
    ] + [sds((2 * KVW, t), bf16)] * z.nc
    scratch = [
        pltpu.VMEM((2 * KVW, z.nc * t), bf16),
        pltpu.VMEM((z.nc * t, t), f32),
        pltpu.VMEM((z.nc, z.rows, t), f32),
        pltpu.VMEM((2 * KVW, z.nc * t), bf16),
    ] + [pltpu.VMEM((QH * HD, t), f32)] * 2
    args = [small, places, q, mid, inv, gain_d, cot_d, mix, lse, cos, sin, own] + list(got) + chunks + pieces
    flops = 10 * z.nc * t * t * QH * HD + 2 * t * z.width**2
    return call(backward_kernel, z, outs, args, scratch, flops)


def qo_weights_kernel(z, n1_ref, mix_ref, dq_ref, midb_ref, gain_two_ref, *refs):
    pieces, (mine_ref, other_ref, nog_ref) = refs[:8], refs[8:]
    at = place()
    fill = jnp.zeros((z.length * z.rows, z.lane - z.qw - 8), f32)
    for fy in (0, 1):
        gain = jnp.concatenate([gathered(z, at, gain_two_ref, fy), fill], axis=1)
        acc = jnp.zeros((z.length * z.rows, z.tokens), f32)
        for piece, fx, fcore in pieces_of(pieces, fy)[::-1]:
            d, out = d_of(at, fx, fcore), other_ref if fcore else mine_ref
            block = jnp.concatenate([nt(n1_ref[fy], dq_ref[d]), gain], axis=1)
            out[fx + 2 * fy, :, : z.lane] = block.astype(bf16)
            out[fx + 2 * fy, :, z.lane :] = nt(mix_ref[fy], midb_ref[d]).astype(bf16)
            acc = acc + nn(piece[:, : z.qw], dq_ref[d])
        nog_ref[fy] = acc


def qo_weights_call(z, n1, mix, dq, midb, gain_two, pieces):
    blocks = (4, z.length * z.rows, z.lane + z.qw)
    outs = [sds(blocks, bf16), sds(blocks, bf16), sds(n1.shape, f32)]
    args = [n1, mix, dq, midb, gain_two] + pieces
    return call(qo_weights_kernel, z, outs, args, (), 6 * z.tokens * z.width**2)


def end_kernel(z, x_ref, inv_ref, gain_ref, n1_ref, midg_ref, nog_ref, cos_ref, sin_ref, own_ref, *refs):
    got, refs = refs[: z.length], refs[z.length :]
    pieces, (grad_ref, mine_ref, other_ref, dkv_ref, u_ref) = refs[:8], refs[8:]
    at = place()
    t, w = z.tokens, 2 * z.kw
    total = own_ref[...].astype(f32)
    for g in got:
        total = total + g[...].astype(f32)
    dk = rotate(total[:KVW], cos_ref[...], -sin_ref[...])
    for d in range(z.nd):
        dkv_ref[d, : z.kw] = dk[z.kw * d : z.kw * (d + 1)].astype(bf16)
        dkv_ref[d, z.kw :] = total[KVW + z.kw * d : KVW + z.kw * (d + 1)].astype(bf16)
    inv = inv_ref[0:1, :]
    mean = jnp.zeros((1, t), f32)
    columns = [(fx, fcore) for _, fx, fcore in pieces_of(pieces, 0)]
    every = jnp.concatenate([dkv_ref[d_of(at, fx, fcore)] for fx, fcore in columns], axis=0)
    for fy in (0, 1):
        nog = nog_ref[fy]
        for k in range(z.length):
            c = c_of(z, at, fy, k)
            block = slice(z.rows * k, z.rows * (k + 1))
            weights = jnp.concatenate([p[k, :w, :] for p, _, _ in pieces_of(pieces, fy)], axis=0)
            acc = nog[block] + tn(weights, every)
            x = x_ref[c].astype(f32)
            row = jnp.sum(jnp.transpose(acc * x * inv), axis=0, keepdims=True)
            gain = jnp.broadcast_to(row, (8, z.rows)).astype(bf16)
            u = acc * gain_ref[c][:, 0:1]
            u_ref[c] = u
            mean = mean + jnp.sum(u * x, axis=0, keepdims=True)
            terms = nt(every, n1_ref[fy][block]).astype(bf16)
            for i, (fx, fcore) in enumerate(columns):
                out = other_ref if fcore else mine_ref
                out[fx + 2 * fy, k, :w] = terms[w * i : w * (i + 1)]
                out[fx + 2 * fy, k, w : w + 8] = gain
    scale = inv * inv * mean * (1.0 / z.width)
    for c in range(z.nc):
        x = x_ref[c].astype(f32)
        grad_ref[c] = midg_ref[c] + inv * (u_ref[c] - x * scale)


def end_call(z, x_c, inv, gain, n1, midg_c, nog, cos, sin, own, got, pieces):
    t = z.tokens
    blocks = (4, z.length, 2 * z.kw + 8, z.rows)
    outs = [sds((z.nc, z.rows, t), f32), sds(blocks, bf16), sds(blocks, bf16)]
    scratch = [pltpu.VMEM((z.nd, 2 * z.kw, t), bf16), pltpu.VMEM((z.nc, z.rows, t), f32)]
    args = [x_c, inv, gain, n1, midg_c, nog, cos, sin, own] + got + pieces
    return call(end_kernel, z, outs, args, scratch, 8 * t * z.width * KVW)


def layer(
    nd, nc, hidden_in, positions, attn_gain, query_w, key_w, value_w, output_w,
    ffn_gain, gate_w, up_w, down_w, cotangent,
):
    _, tokens, width = hidden_in.shape
    z = SimpleNamespace(nd=nd, nc=nc, length=nc // 2, tokens=tokens, width=width, rows=width // nc)
    z.qw, z.kw, z.units = query_w.shape[1], key_w.shape[1], gate_w.shape[1] // 2
    z.down_rows, z.fold = down_w.shape[0], nc // (2 * nd)
    z.lane = -(-(z.qw + 8) // 128) * 128
    z.dt_lane = 2 * z.units if z.fold == 1 else 0
    L, t, rows = z.length, tokens, z.rows
    grad_scale = float(tokens * nd * nc) ** (-0.5)
    y0 = lax.rem(lax.axis_index("ctx"), 2)

    x_t, cot_t = hidden_in[0].T, cotangent[0].T
    x_c, x_d, cot_d = x_t.reshape(nc, rows, t), x_t.reshape(nd, z.qw, t), cot_t.reshape(nd, z.qw, t)

    def along_line(x):
        return [x] + [from_line(z, x, k) for k in range(1, L)]

    def over_slab(x, relay=False):
        mine = [x] + [to_slot(z, x, i) for i in (1, 2)]
        if relay:
            mine += [to_slot(z, mine[2], 1)]
        else:
            mine += [to_slot(z, x, 3)]
        return mine + [to_core(z, p) for p in mine]

    def flat(x):
        return x.reshape((L * x.shape[1],) + x.shape[2:])

    kv_line = along_line(first_call(z, key_w.T, value_w.T, attn_gain, ffn_gain, positions))
    kv_w = over_slab(jnp.stack(kv_line))

    pad = z.lane - z.qw
    qo = jnp.concatenate([jnp.pad(query_w, ((0, 0), (0, pad))), output_w], axis=1)
    qo_line = along_line(qo)
    qo_w = over_slab(flat(jnp.stack(qo_line)), relay=True)

    def own_half(w, other):
        low = (y0 == 0) != other
        return jnp.where(low, w[:, : z.units], w[:, z.units :])

    keep = jnp.concatenate([own_half(gate_w, False), own_half(up_w, False)], axis=1)
    give = jnp.concatenate([own_half(gate_w, True), own_half(up_w, True)], axis=1)
    take = to_slot(z, give, 2)
    gate_up = jnp.where(
        y0 == 0, jnp.concatenate([keep, take], axis=0), jnp.concatenate([take, keep], axis=0)
    )

    def down_target(d, c):
        n, i = c // z.fold, c % z.fold
        return n // 2, 2 * (z.fold * d + i) + n % 2

    down_back = {down_target(d, c): (d, c) for d in range(nd) for c in range(nc)}
    down_t = moved(z, down_w.T, down_target)
    if z.fold == 1:
        gus = line_pieces(z, jnp.concatenate([gate_up, down_t], axis=1))
        dts = gus
    else:
        gus, dts = line_pieces(z, gate_up), line_pieces(z, down_t)

    frequency = jnp.power(rope_base, -2.0 * jnp.arange(HALF, dtype=f32) / HD)
    angles = frequency[:, None] * positions[0].astype(f32)[None, :]
    cos, sin = jnp.cos(angles), jnp.sin(angles)
    places = jnp.broadcast_to(positions[0].astype(f32)[None, :], (8, t))

    kv, n1, inv_one, gain, small = kv_call(z, x_c, cos, sin, kv_w)
    gain_d = gain.reshape(nd, z.qw, 8)
    kv_along = along_line(kv)
    chunks = kv_along + [to_slot(z, p, 2) for p in kv_along]
    q = q_call(z, n1, cos, sin, qo_w)
    mix, mix_rows, lse, mid, inv_two, n2 = forward_call(z, small, places, q, x_d, gain_d, chunks, qo_w)

    cots = over_slab(cot_d, relay=True)
    n2s = over_slab(n2.reshape(width, t))
    ntg_mine, ntg_other, gu, act, n2_all, cot_all = ffn_call(z, n2s, cots, gus, dts)
    ntg_own, *ntg_send = core_sum(ntg_mine, to_core(z, ntg_other))
    ntg_got = [to_slot(z, s, i + 1) for i, s in enumerate(ntg_send)]

    hid_mine, hid_other = hidden_call(z, act, dts)
    hid_own, *hid_send = core_sum(hid_mine, to_core(z, hid_other))
    gu_grads, dt_grads = ffn_weights_call(z, gu, act, n2_all, cot_all)

    midg, midb, gain_two, dq, *dkv = backward_call(
        z, small, places, q, mid, inv_two, gain_d, cot_d, mix_rows, lse, cos, sin,
        ntg_own, ntg_got, chunks, qo_w,
    )

    dkv_got = []
    for k in range(L):
        got = to_slot(z, dkv[L + k], 2)
        if k == 0:
            dkv_got.append(got)
        else:
            both = (dkv[k].astype(f32) + got.astype(f32)).astype(bf16)
            dkv_got.append(from_line(z, both, -k))

    qo_mine, qo_other, nog = qo_weights_call(
        z, n1, mix, dq, midb, gain_two.reshape(nc, rows, 8), qo_w
    )
    grad_in, kv_mine, kv_other = end_call(
        z, x_c, inv_one, gain, n1, midg.reshape(nc, rows, t), nog, cos, sin, dkv[0], dkv_got, kv_w
    )

    def to_owner(mine, other):
        own, *sends = core_sum(mine, to_core(z, other))
        got = [to_slot(z, s, i + 1) for i, s in enumerate(sends)]
        return line_sum(slab_sum(z, own, got))

    def line_sum(pieces):
        total = pieces[0].astype(f32)
        for k in range(1, L):
            total = total + from_line(z, pieces[k], -k).astype(f32)
        return total * grad_scale

    sum_kv = to_owner(kv_mine, kv_other)
    sum_qo = to_owner(qo_mine, qo_other)

    hidden_out = mid + hid_own
    for i, s in enumerate(hid_send):
        hidden_out = hidden_out + to_slot(z, s, i + 1).astype(f32)

    s_gu = line_sum(gu_grads)
    s_dt = s_gu[:, 2 * z.units :] if z.fold == 1 else line_sum(dt_grads)
    s_gu = s_gu[:, : 2 * z.units]
    mine = jnp.where(y0 == 0, s_gu[:rows], s_gu[rows:])
    theirs = jnp.where(y0 == 0, s_gu[rows:], s_gu[:rows]).astype(bf16)
    theirs = to_slot(z, theirs, 2).astype(f32)
    low, high = jnp.where(y0 == 0, mine, theirs), jnp.where(y0 == 0, theirs, mine)
    grad_gate = jnp.concatenate([low[:, : z.units], high[:, : z.units]], axis=1)
    grad_up = jnp.concatenate([low[:, z.units :], high[:, z.units :]], axis=1)
    s_dt = moved(z, s_dt.astype(bf16), lambda d, c: down_back[(d, c)])
    grad_down = s_dt.astype(f32).T

    kw, qw, w = z.kw, z.qw, 2 * z.kw
    return (
        hidden_out.reshape(width, t).T[None],
        grad_in.reshape(width, t).T[None],
        sum_kv[w],
        sum_qo[:, :qw],
        sum_kv[:kw].T,
        sum_kv[kw:w].T,
        sum_qo[:, z.lane :],
        sum_qo[:, qw],
        grad_gate,
        grad_up,
        grad_down,
    )


def solution(mesh):
    nd, nc = mesh.shape["dp"], mesh.shape["ctx"]
    whole, rows, gain = P("dp", "ctx", None), P("ctx", "dp"), P("ctx")
    in_specs = (whole, P("dp", "ctx"), gain, rows, rows, rows, rows, gain, rows, rows, rows, whole)
    out_specs = (whole, whole, gain, rows, rows, rows, rows, gain, rows, rows, rows)
    return jax.shard_map(
        functools.partial(layer, nd, nc),
        mesh=mesh,
        in_specs=in_specs,
        out_specs=out_specs,
        check_vma=False,
    )
```

profile of v0, /device:TPU:0, one launch (start us, length us, event | category | flops | bytes accessed | tf_op | source)
XLA Modules:
  0.0 311.4 jit_solution(4226300014874881835)
XLA Ops:
  17.0 5.6 %collective-permute-start.5 = (bf16[4,168,120]{2,1,0:T(8,128)(2,1)S(1)}, bf16[4,168,120]{2,1,0:T(8,128)(2,1)S(1)}, u32[]{:S(2)}, u32[]{:S(2)}) collective-permute-start(bf16[4,168,120]{2,1,0:T(8,128)(2,1)S(1)} %pad_maximum_fusion.4.refs_0_.refs_4_), channel_id=1, source_target_pairs={{0,17},{1,16},{2,19},{3,18},{4,21},{5,20},{6,23},{7,22},{8,25},{9,... | collective-permute-start | bytes 483848 | tf_op jit(solution)/shard_map/ppermute | solution.py:35
  46.1 4.0 %collective-permute-done.29.refs_3_ = bf16[4,240,128]{2,1,0:T(8,128)(2,1)} collective-permute-done((bf16[4,240,128]{2,1,0:T(8,128)(2,1)}, bf16[4,240,128]{2,1,0:T(8,128)(2,1)}, u32[]{:S(2)}, u32[]{:S(2)}) %collective-permute-start.29) | collective-permute-done | bytes 245792 | tf_op jit(solution)/shard_map/ppermute | solution.py:35
  51.1 6.4 %collective-permute-done.23.refs_4_.refs_7_ = bf16[640,128]{1,0:T(8,128)(2,1)S(1)} collective-permute-done((bf16[640,128]{1,0:T(8,128)(2,1)}, bf16[640,128]{1,0:T(8,128)(2,1)S(1)}, u32[]{:S(2)}, u32[]{:S(2)}) %collective-permute-start.23) | collective-permute-done | bytes 163872 | tf_op jit(solution)/shard_map/ppermute | solution.py:35
  60.4 5.5 %collective-permute-done.21.refs_2_.refs_5_ = bf16[640,128]{1,0:T(8,128)(2,1)} collective-permute-done((bf16[640,128]{1,0:T(8,128)(2,1)}, bf16[640,128]{1,0:T(8,128)(2,1)}, u32[]{:S(2)}, u32[]{:S(2)}) %collective-permute-start.21) | collective-permute-done | bytes 163872 | tf_op jit(solution)/shard_map/ppermute | solution.py:35
  71.4 10.7 %collective-permute-done.37.refs_10_.refs_3_ = bf16[240,960]{1,0:T(8,128)(2,1)S(1)} collective-permute-done((bf16[240,960]{1,0:T(8,128)(2,1)S(1)}, bf16[240,960]{1,0:T(8,128)(2,1)S(1)}, u32[]{:S(2)}, u32[]{:S(2)}) %collective-permute-start.37) | collective-permute-done | bytes 460832 | tf_op jit(solution)/shard_map/ppermute | solution.py:35
  82.6 6.8 %collective-permute-done.36.refs_9_.refs_1_ = bf16[240,960]{1,0:T(8,128)(2,1)S(1)} collective-permute-done((bf16[240,960]{1,0:T(8,128)(2,1)S(1)}, bf16[240,960]{1,0:T(8,128)(2,1)S(1)}, u32[]{:S(2)}, u32[]{:S(2)}) %collective-permute-start.36) | collective-permute-done | bytes 460832 | tf_op jit(solution)/shard_map/ppermute | solution.py:35
  92.4 4.4 %collective-permute-done.25.refs_6_.refs_9_ = bf16[640,128]{1,0:T(8,128)(2,1)} collective-permute-done((bf16[640,128]{1,0:T(8,128)(2,1)}, bf16[640,128]{1,0:T(8,128)(2,1)}, u32[]{:S(2)}, u32[]{:S(2)}) %collective-permute-start.25) | collective-permute-done | bytes 163872 | tf_op jit(solution)/shard_map/ppermute | solution.py:35
  104.4 3.7 %shard_map.205.q_ref = bf16[960,128]{1,0:T(8,128)(2,1)} custom-call(bf16[2,480,128]{2,1,0:T(8,128)(2,1)} %get-tuple-element.56.n1_ref, f32[32,128]{1,0:T(8,128)} %get-tuple-element.161.cos_ref, f32[32,128]{1,0:T(8,128)} %get-tuple-element.160.sin_ref, bf16[480,496]{1,0:T(8,128)(2,1)} %bitcast.204, bf16[480,496]{1,0:T(8,128)(2,1)} %copy-done.3, ...), custom_call_target="tpu_custom_call" | custom-call | flops 235929600 | bytes 4333568 | tf_op jit(solution)/shard_map/pallas_call | solution.py:124
  108.7 9.1 %shard_map.206 = (bf16[2,480,128]{2,1,0:T(8,128)(2,1)}, bf16[960,128]{1,0:T(8,128)(2,1)}, f32[8,384]{1,0:T(8,128)}, f32[4,240,128]{2,1,0:T(8,128)}, f32[8,128]{1,0:T(8,128)}, /*index=5*/bf16[4,240,128]{2,1,0:T(8,128)(2,1)}) custom-call(f32[8,8,120]{2,1,0:T(8,128)} %get-tuple-element.55.small_ref, f32[8,128]{1,0:T(8,128)} %broadcast_in_dim.22.places_ref, ...), custom_call_target="tpu_custom_call" | custom-call | flops 739246080 | bytes 6922240 | tf_op jit(solution)/shard_map/pallas_call | solution.py:124
  121.3 5.4 %shard_map.207 = (bf16[720,960]{1,0:T(8,128)(2,1)}, bf16[640,720]{1,0:T(8,128)(2,1)}, bf16[960,1024]{1,0:T(8,128)(2,1)}, f32[320,1024]{1,0:T(8,128)}) custom-call(bf16[4,240,128]{2,1,0:T(8,128)(2,1)} %bitcast.214, bf16[4,240,128]{2,1,0:T(8,128)(2,1)} %collective-permute-done.27.refs_1_, bf16[4,240,128]{2,1,0:T(8,128)(2,1)} %collective-permute-done.28.refs_2_, ...), custom_call_target="tpu_custom_call" | custom-call | flops 629145600 | bytes 8929280 | tf_op jit(solution)/shard_map/pallas_call | solution.py:124
  127.8 4.4 %collective-permute-done.41.refs_2_ = bf16[960,128]{1,0:T(8,128)(2,1)S(1)} collective-permute-done((bf16[960,128]{1,0:T(8,128)(2,1)}, bf16[960,128]{1,0:T(8,128)(2,1)S(1)}, u32[]{:S(2)}, u32[]{:S(2)}) %collective-permute-start.41) | collective-permute-done | bytes 245792 | tf_op jit(solution)/shard_map/ppermute | solution.py:35
  135.6 8.8 %shard_map.208 = (bf16[4,4,240,128]{3,2,1,0:T(8,128)(2,1)}, bf16[4,4,240,128]{3,2,1,0:T(8,128)(2,1)}, bf16[640,1024]{1,0:T(8,128)(2,1)}, bf16[320,1024]{1,0:T(8,128)(2,1)}, bf16[960,1024]{1,0:T(8,128)(2,1)}) custom-call(bf16[720,960]{1,0:T(8,128)(2,1)} %get-tuple-element.60.w_ref, bf16[640,720]{1,0:T(8,128)(2,1)} %get-tuple-element.61.turned_ref, ...), custom_call_target="tpu_custom_call" | custom-call | flops 3145728000 | bytes 13905920 | tf_op jit(solution)/shard_map/pallas_call | solution.py:124
  144.5 6.6 %shard_map.213 = (bf16[240,960]{1,0:T(8,128)(2,1)}, bf16[240,960]{1,0:T(8,128)(2,1)}, bf16[240,960]{1,0:T(8,128)(2,1)}, bf16[240,960]{1,0:T(8,128)(2,1)}) custom-call(bf16[640,1024]{1,0:T(8,128)(2,1)} %get-tuple-element.93.gu_ref, bf16[320,1024]{1,0:T(8,128)(2,1)} %get-tuple-element.65.act_ref, bf16[960,1024]{1,0:T(8,128)(2,1)} %get-tuple-element.94.n2_ref, ...), custom_call_target="tpu_custom_call" | custom-call | flops 1887436800 | bytes 7741440 | tf_op jit(solution)/shard_map/pallas_call | solution.py:124
  156.9 4.0 %shard_map.209 = (bf16[4,4,240,128]{3,2,1,0:T(8,128)(2,1)}, bf16[4,4,240,128]{3,2,1,0:T(8,128)(2,1)}) custom-call(bf16[320,1024]{1,0:T(8,128)(2,1)} %get-tuple-element.65.act_ref, bf16[240,960]{1,0:T(8,128)(2,1)} %copy-done.7, bf16[240,960]{1,0:T(8,128)(2,1)} %copy-done.9, bf16[240,960]{1,0:T(8,128)(2,1)} %broadcast_select_fusion.2.far_ref.refs_2_, ...), custom_call_target="tpu_custom_call" | custom-call | flops 629145600 | bytes 4464640 | tf_op jit(solution)/shard_map/pallas_call | solution.py:124
  168.8 19.1 %collective-permute-done.77 = bf16[240,960]{1,0:T(8,128)(2,1)S(1)} collective-permute-done((bf16[240,960]{1,0:T(8,128)(2,1)}, bf16[240,960]{1,0:T(8,128)(2,1)S(1)}, u32[]{:S(2)}, u32[]{:S(2)}) %collective-permute-start.77) | collective-permute-done | bytes 460832 | tf_op jit(solution)/shard_map/ppermute | solution.py:35
  191.4 10.9 %shard_map.210 = (f32[4,240,128]{2,1,0:T(8,128)}, bf16[4,240,128]{2,1,0:T(8,128)(2,1)}, f32[4,240,8]{2,1,0:T(8,128)}, bf16[4,240,128]{2,1,0:T(8,128)(2,1)}, bf16...) custom-call(f32[8,8,120]{2,1,0:T(8,128)} %get-tuple-element.55.small, ...), custom_call_target="tpu_custom_call" | custom-call | flops 1494220800 | bytes 10016768 | tf_op jit(solution)/shard_map/pallas_call | solution.py:124
  207.3 6.1 %shard_map.211 = (bf16[4,480,496]{2,1,0:T(8,128)(2,1)}, bf16[4,480,496]{2,1,0:T(8,128)(2,1)}, f32[2,480,128]{2,1,0:T(8,128)}) custom-call(bf16[2,480,128]{2,1,0:T(8,128)(2,1)} %get-tuple-element.56.n1_ref, bf16[2,480,128]{2,1,0:T(8,128)(2,1)} %get-tuple-element.75.mix_ref, bf16[4,240,128]{2,1,0:T(8,128)(2,1)} %get-tuple-element.76.dq_ref, ...), custom_call_target="tpu_custom_call" | custom-call | flops 707788800 | bytes 9123840 | tf_op jit(solution)/shard_map/pallas_call | solution.py:124
  213.5 11.0 %collective-permute-start.69 = (bf16[4,480,496]{2,1,0:T(8,128)(2,1)}, bf16[4,480,496]{2,1,0:T(8,128)(2,1)S(1)}, u32[]{:S(2)}, u32[]{:S(2)}) collective-permute-start(bf16[4,480,496]{2,1,0:T(8,128)(2,1)} %get-tuple-element.92), channel_id=1, source_target_pairs={{0,8},{1,9},{2,10},{3,11},{4,12},{5,13},{6,14},{7,15},{8,0},{9,1},... | collective-permute-start | bytes 5713928 | tf_op jit(solution)/shard_map/ppermute | solution.py:35
  234.5 7.0 %collective-permute-done.59.refs_2_ = bf16[640,128]{1,0:T(8,128)(2,1)S(1)} collective-permute-done((bf16[640,128]{1,0:T(8,128)(2,1)S(1)}, bf16[640,128]{1,0:T(8,128)(2,1)S(1)}, u32[]{:S(2)}, u32[]{:S(2)}) %collective-permute-start.59) | collective-permute-done | bytes 163872 | tf_op jit(solution)/shard_map/ppermute | solution.py:35
  242.7 4.7 %shard_map.212 = (f32[8,120,128]{2,1,0:T(8,128)}, bf16[4,4,168,120]{3,2,1,0:T(8,128)(2,1)}, bf16[4,4,168,120]{3,2,1,0:T(8,128)(2,1)}) custom-call(bf16[8,120,128]{2,1,0:T(8,128)(2,1)} %bitcast.212, f32[8,128]{1,0:T(8,128)} %get-tuple-element.68.inv_ref, f32[8,120,8]{2,1,0:T(8,128)} %get-tuple-element.57.gain_ref, ...), custom_call_target="tpu_custom_call" | custom-call | flops 314572800 | bytes 5433344 | tf_op jit(solution)/shard_map/pallas_call | solution.py:124
  262.9 4.1 %collective-permute-start.66 = (bf16[168,120]{1,0:T(8,128)(2,1)S(1)}, bf16[168,120]{1,0:T(8,128)(2,1)S(1)}, u32[]{:S(2)}, u32[]{:S(2)}) collective-permute-start(bf16[168,120]{1,0:T(8,128)(2,1)S(1)} %get-tuple-element.143), channel_id=1, source_target_pairs={{0,2},{1,3},{2,4},{3,5},{4,6},{5,7},{6,0},{7,1},{8,10},{9,11},{10,... | collective-permute-start | bytes 120968 | tf_op jit(solution)/shard_map/ppermute | solution.py:35
  278.2 7.5 %collective-permute-done.70 = bf16[480,496]{1,0:T(8,128)(2,1)S(1)} collective-permute-done((bf16[480,496]{1,0:T(8,128)(2,1)S(1)}, bf16[480,496]{1,0:T(8,128)(2,1)S(1)}, u32[]{:S(2)}, u32[]{:S(2)}) %collective-permute-start.70) | collective-permute-done | bytes 476192 | tf_op jit(solution)/shard_map/ppermute | solution.py:35
  285.6 10.0 %collective-permute-done.72 = bf16[480,496]{1,0:T(8,128)(2,1)S(1)} collective-permute-done((bf16[480,496]{1,0:T(8,128)(2,1)S(1)}, bf16[480,496]{1,0:T(8,128)(2,1)S(1)}, u32[]{:S(2)}, u32[]{:S(2)}) %collective-permute-start.72) | collective-permute-done | bytes 476192 | tf_op jit(solution)/shard_map/ppermute | solution.py:35
  297.2 4.1 %collective-permute-start.73 = (bf16[120,496]{1,0:T(8,128)(2,1)S(1)}, bf16[120,496]{1,0:T(8,128)(2,1)S(1)}, u32[]{:S(2)}, u32[]{:S(2)}) collective-permute-start(bf16[120,496]{1,0:T(8,128)(2,1)S(1)} %get-tuple-element.125), channel_id=1, source_target_pairs={{0,2},{1,3},{2,4},{3,5},{4,6},{5,7},{6,0},{7,1},{8,10},{9,11},{10,... | collective-permute-start | bytes 357128 | tf_op jit(solution)/shard_map/ppermute | solution.py:35
  (285 shorter events, 140.1 us)
Async XLA Ops:
  38.6 20.7 %collective-permute-start.14 = (bf16[480,496]{1,0:T(8,128)(2,1)S(1)}, bf16[480,496]{1,0:T(8,128)(2,1)S(1)}, u32[]{:S(2)}, u32[]{:S(2)}) collective-permute-start(bf16[480,496]{1,0:T(8,128)(2,1)S(1)} %bitcast.201), channel_id=1, source_target_pairs={{0,1},{1,0},{2,3},{3,2},{4,5},{5,4},{6,7},{7,6},{8,9},{9,8},{10,11... | collective-permute-start | bytes 1428488 | tf_op jit(solution)/shard_map/ppermute | solution.py:35
  46.1 24.6 %collective-permute-start.16 = (bf16[480,496]{1,0:T(8,128)(2,1)S(1)}, bf16[480,496]{1,0:T(8,128)(2,1)S(1)}, u32[]{:S(2)}, u32[]{:S(2)}) collective-permute-start(bf16[480,496]{1,0:T(8,128)(2,1)S(1)} %bitcast.202), channel_id=1, source_target_pairs={{0,8},{1,9},{2,10},{3,11},{4,12},{5,13},{6,14},{7,15},{8,0},{9,1},... | collective-permute-start | bytes 1428488 | tf_op jit(solution)/shard_map/ppermute | solution.py:35
  50.1 20.6 %collective-permute-start.13 = (bf16[480,496]{1,0:T(8,128)(2,1)S(1)}, bf16[480,496]{1,0:T(8,128)(2,1)S(1)}, u32[]{:S(2)}, u32[]{:S(2)}) collective-permute-start(bf16[480,496]{1,0:T(8,128)(2,1)S(1)} %bitcast.203), channel_id=1, source_target_pairs={{0,16},{1,17},{2,18},{3,19},{4,20},{5,21},{6,22},{7,23},{8,24},{9,... | collective-permute-start | bytes 1428488 | tf_op jit(solution)/shard_map/ppermute | solution.py:35
  59.3 22.8 %collective-permute-start.15 = (bf16[480,496]{1,0:T(8,128)(2,1)S(1)}, bf16[480,496]{1,0:T(8,128)(2,1)S(1)}, u32[]{:S(2)}, u32[]{:S(2)}) collective-permute-start(bf16[480,496]{1,0:T(8,128)(2,1)S(1)} %collective-permute-done.14.refs_2_.refs_10_.refs_13_), channel_id=1, source_target_pairs={{0,16},{1,17},{2,18},{3,19},{4,20},{5,21},{6,22},{7,23},{8,24},{9,... | collective-permute-start | bytes 1428488 | tf_op jit(solution)/shard_map/ppermute | solution.py:35
  67.6 21.8 %collective-permute-start.36 = (bf16[240,960]{1,0:T(8,128)(2,1)S(1)}, bf16[240,960]{1,0:T(8,128)(2,1)S(1)}, u32[]{:S(2)}, u32[]{:S(2)}) collective-permute-start(bf16[240,960]{1,0:T(8,128)(2,1)S(1)} %pad_maximum_fusion.1.refs_8_.refs_0_), channel_id=1, source_target_pairs={{0,6},{1,7},{2,0},{3,1},{4,2},{5,3},{6,4},{7,5},{8,14},{9,15},{10,... | collective-permute-start | bytes 1382408 | tf_op jit(solution)/shard_map/ppermute | solution.py:35
  70.7 28.6 %collective-permute-start.18 = (bf16[480,496]{1,0:T(8,128)(2,1)S(1)}, bf16[480,496]{1,0:T(8,128)(2,1)S(1)}, u32[]{:S(2)}, u32[]{:S(2)}) collective-permute-start(bf16[480,496]{1,0:T(8,128)(2,1)S(1)} %collective-permute-done.14.refs_2_.refs_10_.refs_13_), channel_id=1, source_target_pairs={{0,8},{1,9},{2,10},{3,11},{4,12},{5,13},{6,14},{7,15},{8,0},{9,1},... | collective-permute-start | bytes 1428488 | tf_op jit(solution)/shard_map/ppermute | solution.py:35
  70.8 20.2 %collective-permute-start.26 = (bf16[640,128]{1,0:T(8,128)(2,1)S(1)}, bf16[640,128]{1,0:T(8,128)(2,1)S(1)}, u32[]{:S(2)}, u32[]{:S(2)}) collective-permute-start(bf16[640,128]{1,0:T(8,128)(2,1)S(1)} %collective-permute-done.22.refs_3_.refs_6_), channel_id=1, source_target_pairs={{0,1},{1,0},{2,3},{3,2},{4,5},{5,4},{6,7},{7,6},{8,9},{9,8},{10,11... | collective-permute-start | bytes 491528 | tf_op jit(solution)/shard_map/ppermute | solution.py:35
  82.1 20.7 %collective-permute-start.19 = (bf16[480,496]{1,0:T(8,128)(2,1)S(1)}, bf16[480,496]{1,0:T(8,128)(2,1)}, u32[]{:S(2)}, u32[]{:S(2)}) collective-permute-start(bf16[480,496]{1,0:T(8,128)(2,1)S(1)} %collective-permute-done.15.refs_3_.refs_11_.refs_14_), channel_id=1, source_target_pairs={{0,8},{1,9},{2,10},{3,11},{4,12},{5,13},{6,14},{7,15},{8,0},{9,1},... | collective-permute-start | bytes 1428488 | tf_op jit(solution)/shard_map/ppermute | solution.py:35
  96.8 20.9 %collective-permute-start.32 = (bf16[4,240,128]{2,1,0:T(8,128)(2,1)}, bf16[4,240,128]{2,1,0:T(8,128)(2,1)}, u32[]{:S(2)}, u32[]{:S(2)}) collective-permute-start(bf16[4,240,128]{2,1,0:T(8,128)(2,1)} %collective-permute-done.28.refs_2_), channel_id=1, source_target_pairs={{0,8},{1,9},{2,10},{3,11},{4,12},{5,13},{6,14},{7,15},{8,0},{9,1},... | collective-permute-start | bytes 737288 | tf_op jit(solution)/shard_map/ppermute | solution.py:35
  99.4 20.8 %collective-permute-start.31 = (bf16[4,240,128]{2,1,0:T(8,128)(2,1)}, bf16[4,240,128]{2,1,0:T(8,128)(2,1)}, u32[]{:S(2)}, u32[]{:S(2)}) collective-permute-start(bf16[4,240,128]{2,1,0:T(8,128)(2,1)} %collective-permute-done.27.refs_1_), channel_id=1, source_target_pairs={{0,8},{1,9},{2,10},{3,11},{4,12},{5,13},{6,14},{7,15},{8,0},{9,1},... | collective-permute-start | bytes 737288 | tf_op jit(solution)/shard_map/ppermute | solution.py:35
  99.4 21.1 %collective-permute-start.33 = (bf16[4,240,128]{2,1,0:T(8,128)(2,1)}, bf16[4,240,128]{2,1,0:T(8,128)(2,1)}, u32[]{:S(2)}, u32[]{:S(2)}) collective-permute-start(bf16[4,240,128]{2,1,0:T(8,128)(2,1)} %collective-permute-done.29.refs_3_), channel_id=1, source_target_pairs={{0,8},{1,9},{2,10},{3,11},{4,12},{5,13},{6,14},{7,15},{8,0},{9,1},... | collective-permute-start | bytes 737288 | tf_op jit(solution)/shard_map/ppermute | solution.py:35
  102.1 24.6 %collective-permute-start.39 = (bf16[240,960]{1,0:T(8,128)(2,1)}, bf16[240,960]{1,0:T(8,128)(2,1)S(1)}, u32[]{:S(2)}, u32[]{:S(2)}) collective-permute-start(bf16[240,960]{1,0:T(8,128)(2,1)} %get-tuple-element.141), channel_id=1, source_target_pairs={{2,4},{3,5},{4,2},{5,3},{10,12},{11,13},{12,10},{13,11},{18,20},{1... | collective-permute-start | bytes 1382408 | tf_op jit(solution)/shard_map/ppermute | solution.py:61
  102.8 29.9 %collective-permute-start.38 = (bf16[240,960]{1,0:T(8,128)(2,1)}, bf16[240,960]{1,0:T(8,128)(2,1)}, u32[]{:S(2)}, u32[]{:S(2)}) collective-permute-start(bf16[240,960]{1,0:T(8,128)(2,1)} %get-tuple-element.142), channel_id=1, source_target_pairs={{2,0},{3,1},{4,6},{5,7},{10,8},{11,9},{12,14},{13,15},{18,16},{19,... | collective-permute-start | bytes 1382408 | tf_op jit(solution)/shard_map/ppermute | solution.py:61
  153.9 34.0 %collective-permute-start.77 = (bf16[240,960]{1,0:T(8,128)(2,1)}, bf16[240,960]{1,0:T(8,128)(2,1)S(1)}, u32[]{:S(2)}, u32[]{:S(2)}) collective-permute-start(bf16[240,960]{1,0:T(8,128)(2,1)} %get-tuple-element.97), channel_id=1, source_target_pairs={{0,4},{1,5},{2,6},{3,7},{4,0},{5,1},{6,2},{7,3},{8,12},{9,13},{10,... | collective-permute-start | bytes 1382408 | tf_op jit(solution)/shard_map/ppermute | solution.py:35
  154.0 33.9 %collective-permute-start.78 = (bf16[240,960]{1,0:T(8,128)(2,1)}, bf16[240,960]{1,0:T(8,128)(2,1)S(1)}, u32[]{:S(2)}, u32[]{:S(2)}) collective-permute-start(bf16[240,960]{1,0:T(8,128)(2,1)} %get-tuple-element.98), channel_id=1, source_target_pairs={{0,6},{1,7},{2,0},{3,1},{4,2},{5,3},{6,4},{7,5},{8,14},{9,15},{10,... | collective-permute-start | bytes 1382408 | tf_op jit(solution)/shard_map/ppermute | solution.py:35
  162.0 28.6 %collective-permute-start.54 = (bf16[4,240,128]{2,1,0:T(8,128)(2,1)S(1)}, bf16[4,240,128]{2,1,0:T(8,128)(2,1)S(1)}, u32[]{:S(2)}, u32[]{:S(2)}) collective-permute-start(bf16[4,240,128]{2,1,0:T(8,128)(2,1)S(1)} %get-tuple-element.128), channel_id=1, source_target_pairs={{0,17},{1,16},{2,19},{3,18},{4,21},{5,20},{6,23},{7,22},{8,25},{9,... | collective-permute-start | bytes 737288 | tf_op jit(solution)/shard_map/ppermute | solution.py:35
  163.7 26.8 %collective-permute-start.53 = (bf16[4,240,128]{2,1,0:T(8,128)(2,1)S(1)}, bf16[4,240,128]{2,1,0:T(8,128)(2,1)S(1)}, u32[]{:S(2)}, u32[]{:S(2)}) collective-permute-start(bf16[4,240,128]{2,1,0:T(8,128)(2,1)S(1)} %get-tuple-element.129), channel_id=1, source_target_pairs={{0,1},{1,0},{2,3},{3,2},{4,5},{5,4},{6,7},{7,6},{8,9},{9,8},{10,11... | collective-permute-start | bytes 737288 | tf_op jit(solution)/shard_map/ppermute | solution.py:35
  167.4 23.1 %collective-permute-start.52 = (bf16[4,240,128]{2,1,0:T(8,128)(2,1)S(1)}, bf16[4,240,128]{2,1,0:T(8,128)(2,1)S(1)}, u32[]{:S(2)}, u32[]{:S(2)}) collective-permute-start(bf16[4,240,128]{2,1,0:T(8,128)(2,1)S(1)} %get-tuple-element.130), channel_id=1, source_target_pairs={{0,16},{1,17},{2,18},{3,19},{4,20},{5,21},{6,22},{7,23},{8,24},{9,... | collective-permute-start | bytes 737288 | tf_op jit(solution)/shard_map/ppermute | solution.py:35
  189.0 42.0 %collective-permute-start.79 = (bf16[120,640]{1,0:T(8,128)(2,1)S(1)}, bf16[120,640]{1,0:T(8,128)(2,1)S(1)}, u32[]{:S(2)}, u32[]{:S(2)}) collective-permute-start(bf16[120,640]{1,0:T(8,128)(2,1)S(1)} %select_convert_fusion), channel_id=1, source_target_pairs={{0,1},{1,0},{2,3},{3,2},{4,5},{5,4},{6,7},{7,6},{8,9},{9,8},{10,11... | collective-permute-start | bytes 460808 | tf_op jit(solution)/shard_map/ppermute | solution.py:35
  203.9 30.2 %collective-permute-start.55 = (bf16[640,128]{1,0:T(8,128)(2,1)}, bf16[640,128]{1,0:T(8,128)(2,1)S(1)}, u32[]{:S(2)}, u32[]{:S(2)}) collective-permute-start(bf16[640,128]{1,0:T(8,128)(2,1)} %get-tuple-element.81), channel_id=1, source_target_pairs={{0,1},{1,0},{2,3},{3,2},{4,5},{5,4},{6,7},{7,6},{8,9},{9,8},{10,11... | collective-permute-start | bytes 491528 | tf_op jit(solution)/shard_map/ppermute | solution.py:35
  205.9 22.4 %collective-permute-start.60 = (bf16[640,128]{1,0:T(8,128)(2,1)}, bf16[640,128]{1,0:T(8,128)(2,1)S(1)}, u32[]{:S(2)}, u32[]{:S(2)}) collective-permute-start(bf16[640,128]{1,0:T(8,128)(2,1)} %get-tuple-element.87), channel_id=1, source_target_pairs={{0,1},{1,0},{2,3},{3,2},{4,5},{5,4},{6,7},{7,6},{8,9},{9,8},{10,11... | collective-permute-start | bytes 491528 | tf_op jit(solution)/shard_map/ppermute | solution.py:35
  213.5 53.5 %collective-permute-start.69 = (bf16[4,480,496]{2,1,0:T(8,128)(2,1)}, bf16[4,480,496]{2,1,0:T(8,128)(2,1)S(1)}, u32[]{:S(2)}, u32[]{:S(2)}) collective-permute-start(bf16[4,480,496]{2,1,0:T(8,128)(2,1)} %get-tuple-element.92), channel_id=1, source_target_pairs={{0,8},{1,9},{2,10},{3,11},{4,12},{5,13},{6,14},{7,15},{8,0},{9,1},... | collective-permute-start | bytes 5713928 | tf_op jit(solution)/shard_map/ppermute | solution.py:35
  273.6 22.1 %collective-permute-start.72 = (bf16[480,496]{1,0:T(8,128)(2,1)S(1)}, bf16[480,496]{1,0:T(8,128)(2,1)S(1)}, u32[]{:S(2)}, u32[]{:S(2)}) collective-permute-start(bf16[480,496]{1,0:T(8,128)(2,1)S(1)} %get-tuple-element.122), channel_id=1, source_target_pairs={{0,17},{1,16},{2,19},{3,18},{4,21},{5,20},{6,23},{7,22},{8,25},{9,... | collective-permute-start | bytes 1428488 | tf_op jit(solution)/shard_map/ppermute | solution.py:35
  275.9 21.1 %collective-permute-start.71 = (bf16[480,496]{1,0:T(8,128)(2,1)S(1)}, bf16[480,496]{1,0:T(8,128)(2,1)S(1)}, u32[]{:S(2)}, u32[]{:S(2)}) collective-permute-start(bf16[480,496]{1,0:T(8,128)(2,1)S(1)} %get-tuple-element.123), channel_id=1, source_target_pairs={{0,1},{1,0},{2,3},{3,2},{4,5},{5,4},{6,7},{7,6},{8,9},{9,8},{10,11... | collective-permute-start | bytes 1428488 | tf_op jit(solution)/shard_map/ppermute | solution.py:35
  (105 other events, 1186.3 us)
where the time goes:
time: 312 us; the launch traced here: 311 us
  waiting for transfers between devices  116 us (37%)
  starting transfers between devices  107 us (34%)
  Pallas kernels  63.9 us (20%)
  other arithmetic  14.3 us (5%)
  local copies, waits for them, and re-layouts  8.6 us (3%)
    ppermute x79, waiting for transfers between devices, moved(): return lax.ppermute(x, AX, table)  116 us
    ppermute x79, starting transfers between devices, moved(): return lax.ppermute(x, AX, table)  105 us
    pallas_call x11, Pallas kernels, call(): pl.pallas_call(functools.partial(kernel, z), out_shape=tuple(outs), in_sp...  63.9 us
  transfers between devices with their start and end apart: 81, of which 31 were waited for; matrix products, arithmetic and copies ran while one was open for 6% of the time, Pallas kernels for 17%

commit v1 on v0

--- a/solution.py
+++ b/solution.py
@@ -45,33 +45,15 @@
 
 
 def from_line(z, x, k):
+    k = k % z.length
     return moved(z, x, lambda d, c: (d, 2 * ((c // 2 - k) % z.length) + c % 2))
 
 
-def inner(z, x, toward_middle, outward):
-    table = []
-    for d in range(z.nd):
-        for c in range(z.nc):
-            l = c // 2
-            to = {1: 2, 2: 1} if not outward else {1: 0, 2: 3}
-            if outward and toward_middle:
-                to = {0: 1, 3: 2}
-            if l in to:
-                table.append((d * z.nc + c, d * z.nc + 2 * to[l] + c % 2))
-    return lax.ppermute(x, AX, table)
-
-
 def line_pieces(z, x):
-    L = z.length
-    if L != 4:
-        return [x] + [from_line(z, x, k) for k in range(1, L)]
+    if z.length != 4:
+        return [x] + [from_line(z, x, k) for k in range(1, z.length)]
     one, three = from_line(z, x, 1), from_line(z, x, 3)
-    l = lax.axis_index("ctx") // 2
-    out = jnp.where(l == 1, one, three)
-    across = jnp.where(l == 1, three, one)
-    p = inner(z, out, False, True)
-    q = inner(z, across, False, False)
-    return [x, one, jnp.where((l == 0) | (l == 3), p, q), three]
+    return [x, one, from_line(z, one, 1), three]
 
 
 def nt(a, b):
@@ -230,7 +212,7 @@
     row = lax.broadcasted_iota(jnp.int32, (t, t), 0)
     low = row < t // 2
     within = jnp.where(low, row, row - t // 2).astype(f32)
-    places = places_ref[0:1, :]
+    places = places_ref[0:1, :].astype(f32)
     for n, chunk in enumerate(chunks):
         kv_ref[:, t * n : t * (n + 1)] = chunk[...]
         c = c_of(z, at, n // z.length, n % z.length)
@@ -732,14 +714,12 @@
     frequency = jnp.power(rope_base, -2.0 * jnp.arange(HALF, dtype=f32) / HD)
     angles = frequency[:, None] * positions[0].astype(f32)[None, :]
     cos, sin = jnp.cos(angles), jnp.sin(angles)
-    places = jnp.broadcast_to(positions[0].astype(f32)[None, :], (8, t))
-
     kv, n1, inv_one, gain, small = kv_call(z, x_c, cos, sin, kv_w)
     gain_d = gain.reshape(nd, z.qw, 8)
     kv_along = along_line(kv)
     chunks = kv_along + [to_slot(z, p, 2) for p in kv_along]
     q = q_call(z, n1, cos, sin, qo_w)
-    mix, mix_rows, lse, mid, inv_two, n2 = forward_call(z, small, places, q, x_d, gain_d, chunks, qo_w)
+    mix, mix_rows, lse, mid, inv_two, n2 = forward_call(z, small, positions, q, x_d, gain_d, chunks, qo_w)
 
     cots = over_slab(cot_d, relay=True)
     n2s = over_slab(n2.reshape(width, t))
@@ -752,7 +732,7 @@
     gu_grads, dt_grads = ffn_weights_call(z, gu, act, n2_all, cot_all)
 
     midg, midb, gain_two, dq, *dkv = backward_call(
-        z, small, places, q, mid, inv_two, gain_d, cot_d, mix_rows, lse, cos, sin,
+        z, small, positions, q, mid, inv_two, gain_d, cot_d, mix_rows, lse, cos, sin,
         ntg_own, ntg_got, chunks, qo_w,
     )
 
@@ -783,23 +763,32 @@
             total = total + from_line(z, pieces[k], -k).astype(f32)
         return total * grad_scale
 
+    def line_reduce(pieces):
+        if L != 4:
+            return line_sum(pieces)
+        passed = from_line(z, pieces[2], 1)
+        three = (pieces[3].astype(f32) + passed.astype(f32)).astype(bf16)
+        total = pieces[0].astype(f32) + from_line(z, pieces[1], -1).astype(f32)
+        return (total + from_line(z, three, -3).astype(f32)) * grad_scale
+
     sum_kv = to_owner(kv_mine, kv_other)
     sum_qo = to_owner(qo_mine, qo_other)
 
+    hid_got = [to_slot(z, s, i + 1) for i, s in enumerate(hid_send)]
     hidden_out = mid + hid_own
-    for i, s in enumerate(hid_send):
-        hidden_out = hidden_out + to_slot(z, s, i + 1).astype(f32)
-
-    s_gu = line_sum(gu_grads)
-    s_dt = s_gu[:, 2 * z.units :] if z.fold == 1 else line_sum(dt_grads)
+    for g in hid_got:
+        hidden_out = hidden_out + g.astype(f32)
+
+    s_gu = line_reduce(gu_grads)
+    s_dt = s_gu[:, 2 * z.units :] if z.fold == 1 else line_reduce(dt_grads)
     s_gu = s_gu[:, : 2 * z.units]
     mine = jnp.where(y0 == 0, s_gu[:rows], s_gu[rows:])
     theirs = jnp.where(y0 == 0, s_gu[rows:], s_gu[:rows]).astype(bf16)
     theirs = to_slot(z, theirs, 2).astype(f32)
+    s_dt = moved(z, s_dt.astype(bf16), lambda d, c: down_back[(d, c)])
     low, high = jnp.where(y0 == 0, mine, theirs), jnp.where(y0 == 0, theirs, mine)
     grad_gate = jnp.concatenate([low[:, : z.units], high[:, : z.units]], axis=1)
     grad_up = jnp.concatenate([low[:, z.units :], high[:, z.units :]], axis=1)
-    s_dt = moved(z, s_dt.astype(bf16), lambda d, c: down_back[(d, c)])
     grad_down = s_dt.astype(f32).T
 
     kw, qw, w = z.kw, z.qw, 2 * z.kw

time: 312 us -> 297 us (0.952)
  starting transfers between devices: 107 us -> 91.7 us
    ppermute x79 -> x80, starting transfers between devices: 105 us -> 91.7 us  [moved(): return lax.ppermute(x, AX, table)]
    select_n x2 -> x0, other arithmetic: 4.11 us -> none  [the longest x1 2.23 us: line_pieces(): across = jnp.where(l == 1, three, one)]
    ppermute x79 -> x80, waiting for transfers between devices: 116 us -> 116 us  [moved(): return lax.ppermute(x, AX, table)]
  transfers between devices with their start and end apart: 81 -> 80, of which waited for: 31 -> 30; matrix products, arithmetic and copies ran while one was open for 6% -> 6% of each run, Pallas kernels for 17% -> 18%
where the time goes in v1:
time: 297 us
  waiting for transfers between devices  116 us (39%)
  starting transfers between devices  91.7 us (31%)
  Pallas kernels  63.6 us (21%)
  other arithmetic  16.9 us (6%)
  local copies, waits for them, and re-layouts  6.95 us (2%)
    ppermute x80, waiting for transfers between devices, moved(): return lax.ppermute(x, AX, table)  116 us
    ppermute x80, starting transfers between devices, moved(): return lax.ppermute(x, AX, table)  91.7 us
    pallas_call x11, Pallas kernels, call(): pl.pallas_call(functools.partial(kernel, z), out_shape=tuple(outs), in_sp...  63.6 us
  transfers between devices with their start and end apart: 80, of which 30 were waited for; matrix products, arithmetic and copies ran while one was open for 6% of the time, Pallas kernels for 18%

profile of v1, /device:TPU:0, one launch (start us, length us, event | category | flops | bytes accessed | tf_op | source)
XLA Modules:
  0.0 296.5 jit_solution(14217653358280162069)
XLA Ops:
  23.6 10.8 %collective-permute-start.3 = (bf16[4,168,120]{2,1,0:T(8,128)(2,1)S(1)}, bf16[4,168,120]{2,1,0:T(8,128)(2,1)S(1)}, u32[]{:S(2)}, u32[]{:S(2)}) collective-permute-start(bf16[4,168,120]{2,1,0:T(8,128)(2,1)S(1)} %pad_maximum_fusion.4.refs_0_.refs_4_), channel_id=1, source_target_pairs={{0,16},{1,17},{2,18},{3,19},{4,20},{5,21},{6,22},{7,23},{8,24},{9,... | collective-permute-start | bytes 483848 | tf_op jit(solution)/shard_map/ppermute | solution.py:35
  42.8 3.3 %collective-permute-done.14.refs_2_.refs_10_.refs_13_ = bf16[480,496]{1,0:T(8,128)(2,1)S(1)} collective-permute-done((bf16[480,496]{1,0:T(8,128)(2,1)S(1)}, bf16[480,496]{1,0:T(8,128)(2,1)S(1)}, u32[]{:S(2)}, u32[]{:S(2)}) %collective-permute-start.14) | collective-permute-done | bytes 476192 | tf_op jit(solution)/shard_map/ppermute | solution.py:35
  57.1 4.2 %collective-permute-done.22.refs_3_.refs_6_ = bf16[640,128]{1,0:T(8,128)(2,1)S(1)} collective-permute-done((bf16[640,128]{1,0:T(8,128)(2,1)}, bf16[640,128]{1,0:T(8,128)(2,1)S(1)}, u32[]{:S(2)}, u32[]{:S(2)}) %collective-permute-start.22) | collective-permute-done | bytes 163872 | tf_op jit(solution)/shard_map/ppermute | solution.py:35
  61.3 6.5 %collective-permute-done.21.refs_2_.refs_5_ = bf16[640,128]{1,0:T(8,128)(2,1)S(1)} collective-permute-done((bf16[640,128]{1,0:T(8,128)(2,1)}, bf16[640,128]{1,0:T(8,128)(2,1)S(1)}, u32[]{:S(2)}, u32[]{:S(2)}) %collective-permute-start.21) | collective-permute-done | bytes 163872 | tf_op jit(solution)/shard_map/ppermute | solution.py:35
  80.4 3.5 %collective-permute-start.36 = (bf16[240,960]{1,0:T(8,128)(2,1)S(1)}, bf16[240,960]{1,0:T(8,128)(2,1)S(1)}, u32[]{:S(2)}, u32[]{:S(2)}) collective-permute-start(bf16[240,960]{1,0:T(8,128)(2,1)S(1)} %pad_maximum_fusion.1.refs_8_.refs_0_), channel_id=1, source_target_pairs={{0,6},{1,7},{2,0},{3,1},{4,2},{5,3},{6,4},{7,5},{8,14},{9,15},{10,... | collective-permute-start | bytes 1382408 | tf_op jit(solution)/shard_map/ppermute | solution.py:35
  85.9 3.7 %shard_map.205.q_ref = bf16[960,128]{1,0:T(8,128)(2,1)} custom-call(bf16[2,480,128]{2,1,0:T(8,128)(2,1)} %get-tuple-element.56.n1_ref, f32[32,128]{1,0:T(8,128)} %get-tuple-element.159.cos_ref, f32[32,128]{1,0:T(8,128)} %get-tuple-element.158.sin_ref, bf16[480,496]{1,0:T(8,128)(2,1)} %bitcast.204, bf16[480,496]{1,0:T(8,128)(2,1)} %copy-done.2, ...), custom_call_target="tpu_custom_call" | custom-call | flops 235929600 | bytes 4333568 | tf_op jit(solution)/shard_map/pallas_call | solution.py:106
  89.7 9.1 %shard_map.206 = (bf16[2,480,128]{2,1,0:T(8,128)(2,1)}, bf16[960,128]{1,0:T(8,128)(2,1)}, f32[8,384]{1,0:T(8,128)}, f32[4,240,128]{2,1,0:T(8,128)}, f32[8,128]{1,0:T(8,128)}, /*index=5*/bf16[4,240,128]{2,1,0:T(8,128)(2,1)}) custom-call(f32[8,8,120]{2,1,0:T(8,128)} %get-tuple-element.55.small_ref, s32[1,128]{1,0:T(1,128)} %places_ref.5, ...), custom_call_target="tpu_custom_call" | custom-call | flops 739246080 | bytes 6918656 | tf_op jit(solution)/shard_map/pallas_call | solution.py:106
  103.7 5.5 %collective-permute-done.41.refs_3_ = bf16[960,128]{1,0:T(8,128)(2,1)S(1)} collective-permute-done((bf16[960,128]{1,0:T(8,128)(2,1)}, bf16[960,128]{1,0:T(8,128)(2,1)S(1)}, u32[]{:S(2)}, u32[]{:S(2)}) %collective-permute-start.41) | collective-permute-done | bytes 245792 | tf_op jit(solution)/shard_map/ppermute | solution.py:35
  109.2 4.4 %collective-permute-done.40.refs_2_ = bf16[960,128]{1,0:T(8,128)(2,1)S(1)} collective-permute-done((bf16[960,128]{1,0:T(8,128)(2,1)}, bf16[960,128]{1,0:T(8,128)(2,1)S(1)}, u32[]{:S(2)}, u32[]{:S(2)}) %collective-permute-start.40) | collective-permute-done | bytes 245792 | tf_op jit(solution)/shard_map/ppermute | solution.py:35
  114.2 5.5 %shard_map.207 = (bf16[720,960]{1,0:T(8,128)(2,1)}, bf16[640,720]{1,0:T(8,128)(2,1)}, bf16[960,1024]{1,0:T(8,128)(2,1)}, f32[320,1024]{1,0:T(8,128)}) custom-call(bf16[4,240,128]{2,1,0:T(8,128)(2,1)} %bitcast.213, bf16[4,240,128]{2,1,0:T(8,128)(2,1)} %copy-done.40, bf16[4,240,128]{2,1,0:T(8,128)(2,1)} %copy-done.39, bf16[4,240,128]{2,1,0:T(8,128)(2,1)} %copy-done.41, ...), custom_call_target="tpu_custom_call" | custom-call | flops 629145600 | bytes 8929280 | tf_op jit(solution)/shard_map/pallas_call | solution.py:106
  120.8 8.8 %shard_map.208 = (bf16[4,4,240,128]{3,2,1,0:T(8,128)(2,1)}, bf16[4,4,240,128]{3,2,1,0:T(8,128)(2,1)}, bf16[640,1024]{1,0:T(8,128)(2,1)}, bf16[320,1024]{1,0:T(8,128)(2,1)}, bf16[960,1024]{1,0:T(8,128)(2,1)}) custom-call(bf16[720,960]{1,0:T(8,128)(2,1)} %get-tuple-element.60.w_ref, bf16[640,720]{1,0:T(8,128)(2,1)} %get-tuple-element.61.turned_ref, ...), custom_call_target="tpu_custom_call" | custom-call | flops 3145728000 | bytes 13905920 | tf_op jit(solution)/shard_map/pallas_call | solution.py:106
  129.7 6.4 %shard_map.213 = (bf16[240,960]{1,0:T(8,128)(2,1)}, bf16[240,960]{1,0:T(8,128)(2,1)}, bf16[240,960]{1,0:T(8,128)(2,1)}, bf16[240,960]{1,0:T(8,128)(2,1)}) custom-call(bf16[640,1024]{1,0:T(8,128)(2,1)} %get-tuple-element.93.gu_ref, bf16[320,1024]{1,0:T(8,128)(2,1)} %get-tuple-element.65.act_ref, bf16[960,1024]{1,0:T(8,128)(2,1)} %get-tuple-element.94.n2_ref, ...), custom_call_target="tpu_custom_call" | custom-call | flops 1887436800 | bytes 7741440 | tf_op jit(solution)/shard_map/pallas_call | solution.py:106
  138.1 22.3 %collective-permute-done.76 = bf16[240,960]{1,0:T(8,128)(2,1)S(1)} collective-permute-done((bf16[240,960]{1,0:T(8,128)(2,1)}, bf16[240,960]{1,0:T(8,128)(2,1)S(1)}, u32[]{:S(2)}, u32[]{:S(2)}) %collective-permute-start.76) | collective-permute-done | bytes 460832 | tf_op jit(solution)/shard_map/ppermute | solution.py:35
  161.9 4.1 %shard_map.209 = (bf16[4,4,240,128]{3,2,1,0:T(8,128)(2,1)}, bf16[4,4,240,128]{3,2,1,0:T(8,128)(2,1)}) custom-call(bf16[320,1024]{1,0:T(8,128)(2,1)} %get-tuple-element.65.act_ref, bf16[240,960]{1,0:T(8,128)(2,1)} %copy-done.8, bf16[240,960]{1,0:T(8,128)(2,1)} %copy-done.10, bf16[240,960]{1,0:T(8,128)(2,1)} %copy-done.33, bf16[240,960]{1,0:T(8,128)(2,1)} %copy-done.9), custom_call_target="tpu_custom_call" | custom-call | flops 629145600 | bytes 4464640 | tf_op jit(solution)/shard_map/pallas_call | solution.py:106
  170.6 4.0 %collective-permute-done.77 = bf16[240,960]{1,0:T(8,128)(2,1)S(1)} collective-permute-done((bf16[240,960]{1,0:T(8,128)(2,1)S(1)}, bf16[240,960]{1,0:T(8,128)(2,1)S(1)}, u32[]{:S(2)}, u32[]{:S(2)}) %collective-permute-start.77) | collective-permute-done | bytes 460832 | tf_op jit(solution)/shard_map/ppermute | solution.py:35
  176.8 4.8 %collective-permute-done.52.refs_1_ = bf16[4,240,128]{2,1,0:T(8,128)(2,1)S(1)} collective-permute-done((bf16[4,240,128]{2,1,0:T(8,128)(2,1)S(1)}, bf16[4,240,128]{2,1,0:T(8,128)(2,1)S(1)}, u32[]{:S(2)}, u32[]{:S(2)}) %collective-permute-start.52) | collective-permute-done | bytes 245792 | tf_op jit(solution)/shard_map/ppermute | solution.py:35
  182.4 11.0 %shard_map.210 = (f32[4,240,128]{2,1,0:T(8,128)}, bf16[4,240,128]{2,1,0:T(8,128)(2,1)}, f32[4,240,8]{2,1,0:T(8,128)}, bf16[4,240,128]{2,1,0:T(8,128)(2,1)}, bf16...) custom-call(f32[8,8,120]{2,1,0:T(8,128)} %get-tuple-element.55.small, ...), custom_call_target="tpu_custom_call" | custom-call | flops 1494220800 | bytes 10013184 | tf_op jit(solution)/shard_map/pallas_call | solution.py:106
  198.6 6.1 %shard_map.211 = (bf16[4,480,496]{2,1,0:T(8,128)(2,1)}, bf16[4,480,496]{2,1,0:T(8,128)(2,1)}, f32[2,480,128]{2,1,0:T(8,128)}) custom-call(bf16[2,480,128]{2,1,0:T(8,128)(2,1)} %get-tuple-element.56.n1_ref, bf16[2,480,128]{2,1,0:T(8,128)(2,1)} %get-tuple-element.75.mix_ref, bf16[4,240,128]{2,1,0:T(8,128)(2,1)} %get-tuple-element.76.dq_ref, ...), custom_call_target="tpu_custom_call" | custom-call | flops 707788800 | bytes 9123840 | tf_op jit(solution)/shard_map/pallas_call | solution.py:106
  218.1 7.9 %collective-permute-done.58.refs_2_ = bf16[640,128]{1,0:T(8,128)(2,1)S(1)} collective-permute-done((bf16[640,128]{1,0:T(8,128)(2,1)S(1)}, bf16[640,128]{1,0:T(8,128)(2,1)S(1)}, u32[]{:S(2)}, u32[]{:S(2)}) %collective-permute-start.58) | collective-permute-done | bytes 163872 | tf_op jit(solution)/shard_map/ppermute | solution.py:35
  226.7 4.6 %shard_map.212 = (f32[8,120,128]{2,1,0:T(8,128)}, bf16[4,4,168,120]{3,2,1,0:T(8,128)(2,1)}, bf16[4,4,168,120]{3,2,1,0:T(8,128)(2,1)}) custom-call(bf16[8,120,128]{2,1,0:T(8,128)(2,1)} %bitcast.212, f32[8,128]{1,0:T(8,128)} %get-tuple-element.68.inv_ref, f32[8,120,8]{2,1,0:T(8,128)} %get-tuple-element.57.gain_ref, ...), custom_call_target="tpu_custom_call" | custom-call | flops 314572800 | bytes 5433344 | tf_op jit(solution)/shard_map/pallas_call | solution.py:106
  247.5 6.1 %collective-permute-done.63 = bf16[4,168,120]{2,1,0:T(8,128)(2,1)} collective-permute-done((bf16[4,168,120]{2,1,0:T(8,128)(2,1)}, bf16[4,168,120]{2,1,0:T(8,128)(2,1)}, u32[]{:S(2)}, u32[]{:S(2)}) %collective-permute-start.63) | collective-permute-done | bytes 161312 | tf_op jit(solution)/shard_map/ppermute | solution.py:35
  254.6 4.1 %collective-permute-start.65 = (bf16[168,120]{1,0:T(8,128)(2,1)S(1)}, bf16[168,120]{1,0:T(8,128)(2,1)S(1)}, u32[]{:S(2)}, u32[]{:S(2)}) collective-permute-start(bf16[168,120]{1,0:T(8,128)(2,1)S(1)} %get-tuple-element.141), channel_id=1, source_target_pairs={{0,2},{1,3},{2,4},{3,5},{4,6},{5,7},{6,0},{7,1},{8,10},{9,11},{10,... | collective-permute-start | bytes 120968 | tf_op jit(solution)/shard_map/ppermute | solution.py:35
  269.6 6.9 %collective-permute-done.69 = bf16[480,496]{1,0:T(8,128)(2,1)S(1)} collective-permute-done((bf16[480,496]{1,0:T(8,128)(2,1)S(1)}, bf16[480,496]{1,0:T(8,128)(2,1)S(1)}, u32[]{:S(2)}, u32[]{:S(2)}) %collective-permute-start.69) | collective-permute-done | bytes 476192 | tf_op jit(solution)/shard_map/ppermute | solution.py:35
  276.5 6.2 %collective-permute-done.71 = bf16[480,496]{1,0:T(8,128)(2,1)S(1)} collective-permute-done((bf16[480,496]{1,0:T(8,128)(2,1)S(1)}, bf16[480,496]{1,0:T(8,128)(2,1)S(1)}, u32[]{:S(2)}, u32[]{:S(2)}) %collective-permute-start.71) | collective-permute-done | bytes 476192 | tf_op jit(solution)/shard_map/ppermute | solution.py:35
  (313 shorter events, 135.3 us)
Async XLA Ops:
  15.3 20.6 %collective-permute-start.5 = (bf16[4,168,120]{2,1,0:T(8,128)(2,1)S(1)}, bf16[4,168,120]{2,1,0:T(8,128)(2,1)S(1)}, u32[]{:S(2)}, u32[]{:S(2)}) collective-permute-start(bf16[4,168,120]{2,1,0:T(8,128)(2,1)S(1)} %pad_maximum_fusion.4.refs_0_.refs_4_), channel_id=1, source_target_pairs={{0,17},{1,16},{2,19},{3,18},{4,21},{5,20},{6,23},{7,22},{8,25},{9,... | collective-permute-start | bytes 483848 | tf_op jit(solution)/shard_map/ppermute | solution.py:35
  17.8 18.1 %collective-permute-start.4 = (bf16[4,168,120]{2,1,0:T(8,128)(2,1)S(1)}, bf16[4,168,120]{2,1,0:T(8,128)(2,1)S(1)}, u32[]{:S(2)}, u32[]{:S(2)}) collective-permute-start(bf16[4,168,120]{2,1,0:T(8,128)(2,1)S(1)} %pad_maximum_fusion.4.refs_0_.refs_4_), channel_id=1, source_target_pairs={{0,1},{1,0},{2,3},{3,2},{4,5},{5,4},{6,7},{7,6},{8,9},{9,8},{10,11... | collective-permute-start | bytes 483848 | tf_op jit(solution)/shard_map/ppermute | solution.py:35
  42.7 27.0 %collective-permute-start.13 = (bf16[480,496]{1,0:T(8,128)(2,1)S(1)}, bf16[480,496]{1,0:T(8,128)(2,1)S(1)}, u32[]{:S(2)}, u32[]{:S(2)}) collective-permute-start(bf16[480,496]{1,0:T(8,128)(2,1)S(1)} %bitcast.202), channel_id=1, source_target_pairs={{0,16},{1,17},{2,18},{3,19},{4,20},{5,21},{6,22},{7,23},{8,24},{9,... | collective-permute-start | bytes 1428488 | tf_op jit(solution)/shard_map/ppermute | solution.py:35
  46.1 24.1 %collective-permute-start.15 = (bf16[480,496]{1,0:T(8,128)(2,1)S(1)}, bf16[480,496]{1,0:T(8,128)(2,1)S(1)}, u32[]{:S(2)}, u32[]{:S(2)}) collective-permute-start(bf16[480,496]{1,0:T(8,128)(2,1)S(1)} %collective-permute-done.14.refs_2_.refs_10_.refs_13_), channel_id=1, source_target_pairs={{0,16},{1,17},{2,18},{3,19},{4,20},{5,21},{6,22},{7,23},{8,24},{9,... | collective-permute-start | bytes 1428488 | tf_op jit(solution)/shard_map/ppermute | solution.py:35
  52.1 18.3 %collective-permute-start.16 = (bf16[480,496]{1,0:T(8,128)(2,1)S(1)}, bf16[480,496]{1,0:T(8,128)(2,1)S(1)}, u32[]{:S(2)}, u32[]{:S(2)}) collective-permute-start(bf16[480,496]{1,0:T(8,128)(2,1)S(1)} %bitcast.203), channel_id=1, source_target_pairs={{0,8},{1,9},{2,10},{3,11},{4,12},{5,13},{6,14},{7,15},{8,0},{9,1},... | collective-permute-start | bytes 1428488 | tf_op jit(solution)/shard_map/ppermute | solution.py:35
  77.4 24.2 %collective-permute-start.37 = (bf16[240,960]{1,0:T(8,128)(2,1)S(1)}, bf16[240,960]{1,0:T(8,128)(2,1)S(1)}, u32[]{:S(2)}, u32[]{:S(2)}) collective-permute-start(bf16[240,960]{1,0:T(8,128)(2,1)S(1)} %pad_maximum_fusion.1.refs_8_.refs_0_), channel_id=1, source_target_pairs={{0,2},{1,3},{2,4},{3,5},{4,6},{5,7},{6,0},{7,1},{8,10},{9,11},{10,... | collective-permute-start | bytes 1382408 | tf_op jit(solution)/shard_map/ppermute | solution.py:35
  80.4 22.4 %collective-permute-start.36 = (bf16[240,960]{1,0:T(8,128)(2,1)S(1)}, bf16[240,960]{1,0:T(8,128)(2,1)S(1)}, u32[]{:S(2)}, u32[]{:S(2)}) collective-permute-start(bf16[240,960]{1,0:T(8,128)(2,1)S(1)} %pad_maximum_fusion.1.refs_8_.refs_0_), channel_id=1, source_target_pairs={{0,6},{1,7},{2,0},{3,1},{4,2},{5,3},{6,4},{7,5},{8,14},{9,15},{10,... | collective-permute-start | bytes 1382408 | tf_op jit(solution)/shard_map/ppermute | solution.py:35
  102.7 16.9 %collective-permute-start.38 = (bf16[240,960]{1,0:T(8,128)(2,1)S(1)}, bf16[240,960]{1,0:T(8,128)(2,1)S(1)}, u32[]{:S(2)}, u32[]{:S(2)}) collective-permute-start(bf16[240,960]{1,0:T(8,128)(2,1)S(1)} %collective-permute-done.36.refs_9_.refs_1_), channel_id=1, source_target_pairs={{0,6},{1,7},{2,0},{3,1},{4,2},{5,3},{6,4},{7,5},{8,14},{9,15},{10,... | collective-permute-start | bytes 1382408 | tf_op jit(solution)/shard_map/ppermute | solution.py:35
  103.7 16.0 %collective-permute-start.42 = (bf16[960,128]{1,0:T(8,128)(2,1)}, bf16[960,128]{1,0:T(8,128)(2,1)S(1)}, u32[]{:S(2)}, u32[]{:S(2)}) collective-permute-start(bf16[960,128]{1,0:T(8,128)(2,1)} %bitcast.237), channel_id=1, source_target_pairs={{0,8},{1,9},{2,10},{3,11},{4,12},{5,13},{6,14},{7,15},{8,0},{9,1},... | collective-permute-start | bytes 737288 | tf_op jit(solution)/shard_map/ppermute | solution.py:35
  129.6 36.4 %collective-permute-start.50 = (bf16[4,4,240,128]{3,2,1,0:T(8,128)(2,1)}, bf16[4,4,240,128]{3,2,1,0:T(8,128)(2,1)S(1)}, u32[]{:S(2)}, u32[]{:S(2)}) collective-permute-start(bf16[4,4,240,128]{3,2,1,0:T(8,128)(2,1)} %get-tuple-element.73), channel_id=1, source_target_pairs={{0,8},{1,9},{2,10},{3,11},{4,12},{5,13},{6,14},{7,15},{8,0},{9,1},... | collective-permute-start | bytes 2949128 | tf_op jit(solution)/shard_map/ppermute | solution.py:35
  136.0 24.3 %collective-permute-start.76 = (bf16[240,960]{1,0:T(8,128)(2,1)}, bf16[240,960]{1,0:T(8,128)(2,1)S(1)}, u32[]{:S(2)}, u32[]{:S(2)}) collective-permute-start(bf16[240,960]{1,0:T(8,128)(2,1)} %get-tuple-element.98), channel_id=1, source_target_pairs={{0,6},{1,7},{2,0},{3,1},{4,2},{5,3},{6,4},{7,5},{8,14},{9,15},{10,... | collective-permute-start | bytes 1382408 | tf_op jit(solution)/shard_map/ppermute | solution.py:35
  136.1 33.3 %collective-permute-start.75 = (bf16[240,960]{1,0:T(8,128)(2,1)}, bf16[240,960]{1,0:T(8,128)(2,1)S(1)}, u32[]{:S(2)}, u32[]{:S(2)}) collective-permute-start(bf16[240,960]{1,0:T(8,128)(2,1)} %get-tuple-element.96), channel_id=1, source_target_pairs={{0,2},{1,3},{2,4},{3,5},{4,6},{5,7},{6,0},{7,1},{8,10},{9,11},{10,... | collective-permute-start | bytes 1382408 | tf_op jit(solution)/shard_map/ppermute | solution.py:35
  166.0 28.4 %collective-permute-start.46 = (bf16[4,4,240,128]{3,2,1,0:T(8,128)(2,1)}, bf16[4,4,240,128]{3,2,1,0:T(8,128)(2,1)S(1)}, u32[]{:S(2)}, u32[]{:S(2)}) collective-permute-start(bf16[4,4,240,128]{3,2,1,0:T(8,128)(2,1)} %get-tuple-element.67), channel_id=1, source_target_pairs={{0,8},{1,9},{2,10},{3,11},{4,12},{5,13},{6,14},{7,15},{8,0},{9,1},... | collective-permute-start | bytes 2949128 | tf_op jit(solution)/shard_map/ppermute | solution.py:35
  174.8 36.6 %collective-permute-start.78 = (bf16[120,640]{1,0:T(8,128)(2,1)S(1)}, bf16[120,640]{1,0:T(8,128)(2,1)S(1)}, u32[]{:S(2)}, u32[]{:S(2)}) collective-permute-start(bf16[120,640]{1,0:T(8,128)(2,1)S(1)} %select_convert_fusion), channel_id=1, source_target_pairs={{0,1},{1,0},{2,3},{3,2},{4,5},{5,4},{6,7},{7,6},{8,9},{9,8},{10,11... | collective-permute-start | bytes 460808 | tf_op jit(solution)/shard_map/ppermute | solution.py:35
  195.5 19.4 %collective-permute-start.54 = (bf16[640,128]{1,0:T(8,128)(2,1)S(1)}, bf16[640,128]{1,0:T(8,128)(2,1)S(1)}, u32[]{:S(2)}, u32[]{:S(2)}) collective-permute-start(bf16[640,128]{1,0:T(8,128)(2,1)S(1)} %copy-done.61), channel_id=1, source_target_pairs={{0,1},{1,0},{2,3},{3,2},{4,5},{5,4},{6,7},{7,6},{8,9},{9,8},{10,11... | collective-permute-start | bytes 491528 | tf_op jit(solution)/shard_map/ppermute | solution.py:35
  204.7 54.0 %collective-permute-start.68 = (bf16[4,480,496]{2,1,0:T(8,128)(2,1)}, bf16[4,480,496]{2,1,0:T(8,128)(2,1)}, u32[]{:S(2)}, u32[]{:S(2)}) collective-permute-start(bf16[4,480,496]{2,1,0:T(8,128)(2,1)} %get-tuple-element.92), channel_id=1, source_target_pairs={{0,8},{1,9},{2,10},{3,11},{4,12},{5,13},{6,14},{7,15},{8,0},{9,1},... | collective-permute-start | bytes 5713928 | tf_op jit(solution)/shard_map/ppermute | solution.py:35
  210.3 15.7 %collective-permute-start.58 = (bf16[640,128]{1,0:T(8,128)(2,1)S(1)}, bf16[640,128]{1,0:T(8,128)(2,1)S(1)}, u32[]{:S(2)}, u32[]{:S(2)}) collective-permute-start(bf16[640,128]{1,0:T(8,128)(2,1)S(1)} %add_convert_fusion.14), channel_id=1, source_target_pairs={{0,4},{1,5},{2,6},{3,7},{4,0},{5,1},{6,2},{7,3},{8,12},{9,13},{10,... | collective-permute-start | bytes 491528 | tf_op jit(solution)/shard_map/ppermute | solution.py:35
  214.9 16.8 %collective-permute-start.79 = (bf16[240,320]{1,0:T(8,128)(2,1)S(1)}, bf16[240,320]{1,0:T(8,128)(2,1)S(1)}, u32[]{:S(2)}, u32[]{:S(2)}) collective-permute-start(bf16[240,320]{1,0:T(8,128)(2,1)S(1)} %slice.600), channel_id=1, source_target_pairs={{0,0},{1,1},{2,8},{3,9},{4,16},{5,17},{6,24},{7,25},{8,2},{9,3},{1... | collective-permute-start | bytes 460808 | tf_op jit(solution)/shard_map/ppermute | solution.py:35
  215.8 45.0 %collective-permute-start.47 = (bf16[4,240,128]{2,1,0:T(8,128)(2,1)}, bf16[4,240,128]{2,1,0:T(8,128)(2,1)}, u32[]{:S(2)}, u32[]{:S(2)}) collective-permute-start(bf16[4,240,128]{2,1,0:T(8,128)(2,1)} %get-tuple-element.132), channel_id=1, source_target_pairs={{0,16},{1,17},{2,18},{3,19},{4,20},{5,21},{6,22},{7,23},{8,24},{9,... | collective-permute-start | bytes 737288 | tf_op jit(solution)/shard_map/ppermute | solution.py:35
  237.1 16.5 %collective-permute-start.63 = (bf16[4,168,120]{2,1,0:T(8,128)(2,1)}, bf16[4,168,120]{2,1,0:T(8,128)(2,1)}, u32[]{:S(2)}, u32[]{:S(2)}) collective-permute-start(bf16[4,168,120]{2,1,0:T(8,128)(2,1)} %get-tuple-element.137), channel_id=1, source_target_pairs={{0,1},{1,0},{2,3},{3,2},{4,5},{5,4},{6,7},{7,6},{8,9},{9,8},{10,11... | collective-permute-start | bytes 483848 | tf_op jit(solution)/shard_map/ppermute | solution.py:35
  242.3 20.1 %collective-permute-start.49 = (bf16[4,240,128]{2,1,0:T(8,128)(2,1)S(1)}, bf16[4,240,128]{2,1,0:T(8,128)(2,1)S(1)}, u32[]{:S(2)}, u32[]{:S(2)}) collective-permute-start(bf16[4,240,128]{2,1,0:T(8,128)(2,1)S(1)} %get-tuple-element.133), channel_id=1, source_target_pairs={{0,17},{1,16},{2,19},{3,18},{4,21},{5,20},{6,23},{7,22},{8,25},{9,... | collective-permute-start | bytes 737288 | tf_op jit(solution)/shard_map/ppermute | solution.py:35
  246.4 16.8 %collective-permute-start.48 = (bf16[4,240,128]{2,1,0:T(8,128)(2,1)S(1)}, bf16[4,240,128]{2,1,0:T(8,128)(2,1)S(1)}, u32[]{:S(2)}, u32[]{:S(2)}) collective-permute-start(bf16[4,240,128]{2,1,0:T(8,128)(2,1)S(1)} %get-tuple-element.134), channel_id=1, source_target_pairs={{0,1},{1,0},{2,3},{3,2},{4,5},{5,4},{6,7},{7,6},{8,9},{9,8},{10,11... | collective-permute-start | bytes 737288 | tf_op jit(solution)/shard_map/ppermute | solution.py:35
  263.3 19.4 %collective-permute-start.71 = (bf16[480,496]{1,0:T(8,128)(2,1)S(1)}, bf16[480,496]{1,0:T(8,128)(2,1)S(1)}, u32[]{:S(2)}, u32[]{:S(2)}) collective-permute-start(bf16[480,496]{1,0:T(8,128)(2,1)S(1)} %get-tuple-element.122), channel_id=1, source_target_pairs={{0,17},{1,16},{2,19},{3,18},{4,21},{5,20},{6,23},{7,22},{8,25},{9,... | collective-permute-start | bytes 1428488 | tf_op jit(solution)/shard_map/ppermute | solution.py:35
  265.0 19.1 %collective-permute-start.70 = (bf16[480,496]{1,0:T(8,128)(2,1)S(1)}, bf16[480,496]{1,0:T(8,128)(2,1)S(1)}, u32[]{:S(2)}, u32[]{:S(2)}) collective-permute-start(bf16[480,496]{1,0:T(8,128)(2,1)S(1)} %get-tuple-element.123), channel_id=1, source_target_pairs={{0,1},{1,0},{2,3},{3,2},{4,5},{5,4},{6,7},{7,6},{8,9},{9,8},{10,11... | collective-permute-start | bytes 1428488 | tf_op jit(solution)/shard_map/ppermute | solution.py:35
  (120 other events, 1460.9 us)

commit v2 on v1

--- a/solution.py
+++ b/solution.py
@@ -225,8 +225,12 @@
     return jnp.concatenate([head_of(ref, GRP * h + g) for g in range(GRP)], axis=1)
 
 
+def scaled(q3):
+    return (q3.astype(f32) * (HD**-0.5)).astype(bf16)
+
+
 def scores(kv_ref, bias_ref, h, q3):
-    s = tn(head_of(kv_ref, h), q3) * (HD**-0.5)
+    s = tn(head_of(kv_ref, h), q3)
     bias = bias_ref[...]
     return s + jnp.concatenate([bias] * GRP, axis=1)
 
@@ -259,7 +263,7 @@
     lay_keys(z, at, chunks, small_ref, places_ref, kv_ref, bias_ref)
 
     def head(h):
-        s = scores(kv_ref, bias_ref, h, three(q_ref, h))
+        s = scores(kv_ref, bias_ref, h, scaled(three(q_ref, h)))
         top = jnp.max(s, axis=0, keepdims=True)
         e = jnp.exp(s - top)
         total = jnp.sum(e, axis=0, keepdims=True)
@@ -536,14 +540,14 @@
     factor = HD**-0.5
 
     def head(h):
-        q3 = three(q_ref, h)
+        q3 = scaled(three(q_ref, h))
         g3 = three(rows_ref, h).astype(bf16)
         delta = jnp.sum(g3.astype(f32) * three(mix_ref, h).astype(f32), axis=0, keepdims=True)
         key, value = head_of(kv_ref, h), head_of(kv_ref, KVH + h)
         p = jnp.exp(scores(kv_ref, bias_ref, h, q3) - lse_ref[pl.ds(h, 1), :])
         dv = nt(g3, p.astype(bf16))
         ds = (p * (tn(value, g3) - delta)).astype(bf16)
-        dk = nt(q3, ds) * factor
+        dk = nt(q3, ds)
         dq = nn(key, ds) * factor
         put_head(dk_ref, h, dk.astype(bf16))
         put_head(dk_ref, KVH + h, dv.astype(bf16))
@@ -758,9 +762,10 @@
         return line_sum(slab_sum(z, own, got))
 
     def line_sum(pieces):
+        got = [from_line(z, pieces[k], -k) for k in range(1, L)]
         total = pieces[0].astype(f32)
-        for k in range(1, L):
-            total = total + from_line(z, pieces[k], -k).astype(f32)
+        for g in got:
+            total = total + g.astype(f32)
         return total * grad_scale
 
     def line_reduce(pieces):
@@ -773,6 +778,7 @@
 
     sum_kv = to_owner(kv_mine, kv_other)
     sum_qo = to_owner(qo_mine, qo_other)
+    grad_query, grad_out, grad_ffn_gain = sum_qo[:, : z.qw], sum_qo[:, z.lane :], sum_qo[:, z.qw]
 
     hid_got = [to_slot(z, s, i + 1) for i, s in enumerate(hid_send)]
     hidden_out = mid + hid_own
@@ -791,16 +797,16 @@
     grad_up = jnp.concatenate([low[:, z.units :], high[:, z.units :]], axis=1)
     grad_down = s_dt.astype(f32).T
 
-    kw, qw, w = z.kw, z.qw, 2 * z.kw
+    kw, w = z.kw, 2 * z.kw
     return (
         hidden_out.reshape(width, t).T[None],
         grad_in.reshape(width, t).T[None],
         sum_kv[w],
-        sum_qo[:, :qw],
+        grad_query,
         sum_kv[:kw].T,
         sum_kv[kw:w].T,
-        sum_qo[:, z.lane :],
-        sum_qo[:, qw],
+        grad_out,
+        grad_ffn_gain,
         grad_gate,
         grad_up,
         grad_down,

time: 297 us -> 297 us (level)
  starting transfers between devices: 91.7 us -> 94.7 us
  waiting for transfers between devices: 116 us -> 113 us
    ppermute x80, waiting for transfers between devices: 116 us -> 113 us  [moved(): return lax.ppermute(x, AX, table)]
    ppermute x80, starting transfers between devices: 91.7 us -> 94.7 us  [moved(): return lax.ppermute(x, AX, table)]
where the time goes in v2:
time: 297 us; the launch traced here: 296 us
  waiting for transfers between devices  113 us (38%)
  starting transfers between devices  94.7 us (32%)
  Pallas kernels  63.4 us (21%)
  other arithmetic  16.9 us (6%)
  local copies, waits for them, and re-layouts  6.95 us (2%)
    ppermute x80, waiting for transfers between devices, moved(): return lax.ppermute(x, AX, table)  113 us
    ppermute x80, starting transfers between devices, moved(): return lax.ppermute(x, AX, table)  94.7 us
    pallas_call x11, Pallas kernels, call(): pl.pallas_call(functools.partial(kernel, z), out_shape=tuple(outs), in_sp...  63.4 us
  transfers between devices with their start and end apart: 80, of which 30 were waited for; matrix products, arithmetic and copies ran while one was open for 6% of the time, Pallas kernels for 18%

profile of v2, /device:TPU:0, one launch (start us, length us, event | category | flops | bytes accessed | tf_op | source)
XLA Modules:
  0.0 296.3 jit_solution(15656152803124396640)
XLA Ops:
  23.6 10.8 %collective-permute-start.3 = (bf16[4,168,120]{2,1,0:T(8,128)(2,1)S(1)}, bf16[4,168,120]{2,1,0:T(8,128)(2,1)S(1)}, u32[]{:S(2)}, u32[]{:S(2)}) collective-permute-start(bf16[4,168,120]{2,1,0:T(8,128)(2,1)S(1)} %pad_maximum_fusion.4.refs_0_.refs_4_), channel_id=1, source_target_pairs={{0,16},{1,17},{2,18},{3,19},{4,20},{5,21},{6,22},{7,23},{8,24},{9,... | collective-permute-start | bytes 483848 | tf_op jit(solution)/shard_map/ppermute | solution.py:35
  42.8 3.3 %collective-permute-done.14.refs_2_.refs_10_.refs_13_ = bf16[480,496]{1,0:T(8,128)(2,1)S(1)} collective-permute-done((bf16[480,496]{1,0:T(8,128)(2,1)S(1)}, bf16[480,496]{1,0:T(8,128)(2,1)S(1)}, u32[]{:S(2)}, u32[]{:S(2)}) %collective-permute-start.14) | collective-permute-done | bytes 476192 | tf_op jit(solution)/shard_map/ppermute | solution.py:35
  57.1 4.2 %collective-permute-done.22.refs_3_.refs_6_ = bf16[640,128]{1,0:T(8,128)(2,1)S(1)} collective-permute-done((bf16[640,128]{1,0:T(8,128)(2,1)}, bf16[640,128]{1,0:T(8,128)(2,1)S(1)}, u32[]{:S(2)}, u32[]{:S(2)}) %collective-permute-start.22) | collective-permute-done | bytes 163872 | tf_op jit(solution)/shard_map/ppermute | solution.py:35
  61.3 6.5 %collective-permute-done.21.refs_2_.refs_5_ = bf16[640,128]{1,0:T(8,128)(2,1)S(1)} collective-permute-done((bf16[640,128]{1,0:T(8,128)(2,1)}, bf16[640,128]{1,0:T(8,128)(2,1)S(1)}, u32[]{:S(2)}, u32[]{:S(2)}) %collective-permute-start.21) | collective-permute-done | bytes 163872 | tf_op jit(solution)/shard_map/ppermute | solution.py:35
  80.4 3.5 %collective-permute-start.36 = (bf16[240,960]{1,0:T(8,128)(2,1)S(1)}, bf16[240,960]{1,0:T(8,128)(2,1)S(1)}, u32[]{:S(2)}, u32[]{:S(2)}) collective-permute-start(bf16[240,960]{1,0:T(8,128)(2,1)S(1)} %pad_maximum_fusion.1.refs_8_.refs_0_), channel_id=1, source_target_pairs={{0,6},{1,7},{2,0},{3,1},{4,2},{5,3},{6,4},{7,5},{8,14},{9,15},{10,... | collective-permute-start | bytes 1382408 | tf_op jit(solution)/shard_map/ppermute | solution.py:35
  85.9 3.7 %shard_map.205.q_ref = bf16[960,128]{1,0:T(8,128)(2,1)} custom-call(bf16[2,480,128]{2,1,0:T(8,128)(2,1)} %get-tuple-element.56.n1_ref, f32[32,128]{1,0:T(8,128)} %get-tuple-element.159.cos_ref, f32[32,128]{1,0:T(8,128)} %get-tuple-element.158.sin_ref, bf16[480,496]{1,0:T(8,128)(2,1)} %bitcast.204, bf16[480,496]{1,0:T(8,128)(2,1)} %copy-done.2, ...), custom_call_target="tpu_custom_call" | custom-call | flops 235929600 | bytes 4333568 | tf_op jit(solution)/shard_map/pallas_call | solution.py:106
  89.7 9.0 %shard_map.206 = (bf16[2,480,128]{2,1,0:T(8,128)(2,1)}, bf16[960,128]{1,0:T(8,128)(2,1)}, f32[8,384]{1,0:T(8,128)}, f32[4,240,128]{2,1,0:T(8,128)}, f32[8,128]{1,0:T(8,128)}, /*index=5*/bf16[4,240,128]{2,1,0:T(8,128)(2,1)}) custom-call(f32[8,8,120]{2,1,0:T(8,128)} %get-tuple-element.55.small_ref, s32[1,128]{1,0:T(1,128)} %places_ref.5, ...), custom_call_target="tpu_custom_call" | custom-call | flops 739246080 | bytes 6918656 | tf_op jit(solution)/shard_map/pallas_call | solution.py:106
  103.7 5.5 %collective-permute-done.41.refs_3_ = bf16[960,128]{1,0:T(8,128)(2,1)S(1)} collective-permute-done((bf16[960,128]{1,0:T(8,128)(2,1)}, bf16[960,128]{1,0:T(8,128)(2,1)S(1)}, u32[]{:S(2)}, u32[]{:S(2)}) %collective-permute-start.41) | collective-permute-done | bytes 245792 | tf_op jit(solution)/shard_map/ppermute | solution.py:35
  109.2 4.4 %collective-permute-done.40.refs_2_ = bf16[960,128]{1,0:T(8,128)(2,1)S(1)} collective-permute-done((bf16[960,128]{1,0:T(8,128)(2,1)}, bf16[960,128]{1,0:T(8,128)(2,1)S(1)}, u32[]{:S(2)}, u32[]{:S(2)}) %collective-permute-start.40) | collective-permute-done | bytes 245792 | tf_op jit(solution)/shard_map/ppermute | solution.py:35
  114.1 5.5 %shard_map.207 = (bf16[720,960]{1,0:T(8,128)(2,1)}, bf16[640,720]{1,0:T(8,128)(2,1)}, bf16[960,1024]{1,0:T(8,128)(2,1)}, f32[320,1024]{1,0:T(8,128)}) custom-call(bf16[4,240,128]{2,1,0:T(8,128)(2,1)} %bitcast.213, bf16[4,240,128]{2,1,0:T(8,128)(2,1)} %copy-done.40, bf16[4,240,128]{2,1,0:T(8,128)(2,1)} %copy-done.39, bf16[4,240,128]{2,1,0:T(8,128)(2,1)} %copy-done.41, ...), custom_call_target="tpu_custom_call" | custom-call | flops 629145600 | bytes 8929280 | tf_op jit(solution)/shard_map/pallas_call | solution.py:106
  120.8 8.8 %shard_map.208 = (bf16[4,4,240,128]{3,2,1,0:T(8,128)(2,1)}, bf16[4,4,240,128]{3,2,1,0:T(8,128)(2,1)}, bf16[640,1024]{1,0:T(8,128)(2,1)}, bf16[320,1024]{1,0:T(8,128)(2,1)}, bf16[960,1024]{1,0:T(8,128)(2,1)}) custom-call(bf16[720,960]{1,0:T(8,128)(2,1)} %get-tuple-element.60.w_ref, bf16[640,720]{1,0:T(8,128)(2,1)} %get-tuple-element.61.turned_ref, ...), custom_call_target="tpu_custom_call" | custom-call | flops 3145728000 | bytes 13905920 | tf_op jit(solution)/shard_map/pallas_call | solution.py:106
  129.6 6.4 %shard_map.213 = (bf16[240,960]{1,0:T(8,128)(2,1)}, bf16[240,960]{1,0:T(8,128)(2,1)}, bf16[240,960]{1,0:T(8,128)(2,1)}, bf16[240,960]{1,0:T(8,128)(2,1)}) custom-call(bf16[640,1024]{1,0:T(8,128)(2,1)} %get-tuple-element.93.gu_ref, bf16[320,1024]{1,0:T(8,128)(2,1)} %get-tuple-element.65.act_ref, bf16[960,1024]{1,0:T(8,128)(2,1)} %get-tuple-element.94.n2_ref, ...), custom_call_target="tpu_custom_call" | custom-call | flops 1887436800 | bytes 7741440 | tf_op jit(solution)/shard_map/pallas_call | solution.py:106
  138.0 22.3 %collective-permute-done.76 = bf16[240,960]{1,0:T(8,128)(2,1)S(1)} collective-permute-done((bf16[240,960]{1,0:T(8,128)(2,1)}, bf16[240,960]{1,0:T(8,128)(2,1)S(1)}, u32[]{:S(2)}, u32[]{:S(2)}) %collective-permute-start.76) | collective-permute-done | bytes 460832 | tf_op jit(solution)/shard_map/ppermute | solution.py:35
  161.9 4.1 %shard_map.209 = (bf16[4,4,240,128]{3,2,1,0:T(8,128)(2,1)}, bf16[4,4,240,128]{3,2,1,0:T(8,128)(2,1)}) custom-call(bf16[320,1024]{1,0:T(8,128)(2,1)} %get-tuple-element.65.act_ref, bf16[240,960]{1,0:T(8,128)(2,1)} %copy-done.8, bf16[240,960]{1,0:T(8,128)(2,1)} %copy-done.10, bf16[240,960]{1,0:T(8,128)(2,1)} %copy-done.33, bf16[240,960]{1,0:T(8,128)(2,1)} %copy-done.9), custom_call_target="tpu_custom_call" | custom-call | flops 629145600 | bytes 4464640 | tf_op jit(solution)/shard_map/pallas_call | solution.py:106
  170.5 4.0 %collective-permute-done.77 = bf16[240,960]{1,0:T(8,128)(2,1)S(1)} collective-permute-done((bf16[240,960]{1,0:T(8,128)(2,1)S(1)}, bf16[240,960]{1,0:T(8,128)(2,1)S(1)}, u32[]{:S(2)}, u32[]{:S(2)}) %collective-permute-start.77) | collective-permute-done | bytes 460832 | tf_op jit(solution)/shard_map/ppermute | solution.py:35
  176.8 4.8 %collective-permute-done.52.refs_1_ = bf16[4,240,128]{2,1,0:T(8,128)(2,1)S(1)} collective-permute-done((bf16[4,240,128]{2,1,0:T(8,128)(2,1)S(1)}, bf16[4,240,128]{2,1,0:T(8,128)(2,1)S(1)}, u32[]{:S(2)}, u32[]{:S(2)}) %collective-permute-start.52) | collective-permute-done | bytes 245792 | tf_op jit(solution)/shard_map/ppermute | solution.py:35
  182.4 10.8 %shard_map.210 = (f32[4,240,128]{2,1,0:T(8,128)}, bf16[4,240,128]{2,1,0:T(8,128)(2,1)}, f32[4,240,8]{2,1,0:T(8,128)}, bf16[4,240,128]{2,1,0:T(8,128)(2,1)}, bf16...) custom-call(f32[8,8,120]{2,1,0:T(8,128)} %get-tuple-element.55.small, ...), custom_call_target="tpu_custom_call" | custom-call | flops 1494220800 | bytes 10013184 | tf_op jit(solution)/shard_map/pallas_call | solution.py:106
  198.4 6.1 %shard_map.211 = (bf16[4,480,496]{2,1,0:T(8,128)(2,1)}, bf16[4,480,496]{2,1,0:T(8,128)(2,1)}, f32[2,480,128]{2,1,0:T(8,128)}) custom-call(bf16[2,480,128]{2,1,0:T(8,128)(2,1)} %get-tuple-element.56.n1_ref, bf16[2,480,128]{2,1,0:T(8,128)(2,1)} %get-tuple-element.75.mix_ref, bf16[4,240,128]{2,1,0:T(8,128)(2,1)} %get-tuple-element.76.dq_ref, ...), custom_call_target="tpu_custom_call" | custom-call | flops 707788800 | bytes 9123840 | tf_op jit(solution)/shard_map/pallas_call | solution.py:106
  217.9 7.9 %collective-permute-done.58.refs_2_ = bf16[640,128]{1,0:T(8,128)(2,1)S(1)} collective-permute-done((bf16[640,128]{1,0:T(8,128)(2,1)S(1)}, bf16[640,128]{1,0:T(8,128)(2,1)S(1)}, u32[]{:S(2)}, u32[]{:S(2)}) %collective-permute-start.58) | collective-permute-done | bytes 163872 | tf_op jit(solution)/shard_map/ppermute | solution.py:35
  226.5 4.6 %shard_map.212 = (f32[8,120,128]{2,1,0:T(8,128)}, bf16[4,4,168,120]{3,2,1,0:T(8,128)(2,1)}, bf16[4,4,168,120]{3,2,1,0:T(8,128)(2,1)}) custom-call(bf16[8,120,128]{2,1,0:T(8,128)(2,1)} %bitcast.212, f32[8,128]{1,0:T(8,128)} %get-tuple-element.68.inv_ref, f32[8,120,8]{2,1,0:T(8,128)} %get-tuple-element.57.gain_ref, ...), custom_call_target="tpu_custom_call" | custom-call | flops 314572800 | bytes 5433344 | tf_op jit(solution)/shard_map/pallas_call | solution.py:106
  247.3 4.7 %collective-permute-done.63 = bf16[4,168,120]{2,1,0:T(8,128)(2,1)} collective-permute-done((bf16[4,168,120]{2,1,0:T(8,128)(2,1)}, bf16[4,168,120]{2,1,0:T(8,128)(2,1)}, u32[]{:S(2)}, u32[]{:S(2)}) %collective-permute-start.63) | collective-permute-done | bytes 161312 | tf_op jit(solution)/shard_map/ppermute | solution.py:35
  253.0 5.5 %collective-permute-start.65 = (bf16[168,120]{1,0:T(8,128)(2,1)S(1)}, bf16[168,120]{1,0:T(8,128)(2,1)S(1)}, u32[]{:S(2)}, u32[]{:S(2)}) collective-permute-start(bf16[168,120]{1,0:T(8,128)(2,1)S(1)} %get-tuple-element.141), channel_id=1, source_target_pairs={{0,2},{1,3},{2,4},{3,5},{4,6},{5,7},{6,0},{7,1},{8,10},{9,11},{10,... | collective-permute-start | bytes 120968 | tf_op jit(solution)/shard_map/ppermute | solution.py:35
  269.4 6.9 %collective-permute-done.69 = bf16[480,496]{1,0:T(8,128)(2,1)S(1)} collective-permute-done((bf16[480,496]{1,0:T(8,128)(2,1)S(1)}, bf16[480,496]{1,0:T(8,128)(2,1)S(1)}, u32[]{:S(2)}, u32[]{:S(2)}) %collective-permute-start.69) | collective-permute-done | bytes 476192 | tf_op jit(solution)/shard_map/ppermute | solution.py:35
  276.3 6.2 %collective-permute-done.71 = bf16[480,496]{1,0:T(8,128)(2,1)S(1)} collective-permute-done((bf16[480,496]{1,0:T(8,128)(2,1)S(1)}, bf16[480,496]{1,0:T(8,128)(2,1)S(1)}, u32[]{:S(2)}, u32[]{:S(2)}) %collective-permute-start.71) | collective-permute-done | bytes 476192 | tf_op jit(solution)/shard_map/ppermute | solution.py:35
  (313 shorter events, 135.3 us)
Async XLA Ops:
  15.3 20.6 %collective-permute-start.5 = (bf16[4,168,120]{2,1,0:T(8,128)(2,1)S(1)}, bf16[4,168,120]{2,1,0:T(8,128)(2,1)S(1)}, u32[]{:S(2)}, u32[]{:S(2)}) collective-permute-start(bf16[4,168,120]{2,1,0:T(8,128)(2,1)S(1)} %pad_maximum_fusion.4.refs_0_.refs_4_), channel_id=1, source_target_pairs={{0,17},{1,16},{2,19},{3,18},{4,21},{5,20},{6,23},{7,22},{8,25},{9,... | collective-permute-start | bytes 483848 | tf_op jit(solution)/shard_map/ppermute | solution.py:35
  17.8 18.1 %collective-permute-start.4 = (bf16[4,168,120]{2,1,0:T(8,128)(2,1)S(1)}, bf16[4,168,120]{2,1,0:T(8,128)(2,1)S(1)}, u32[]{:S(2)}, u32[]{:S(2)}) collective-permute-start(bf16[4,168,120]{2,1,0:T(8,128)(2,1)S(1)} %pad_maximum_fusion.4.refs_0_.refs_4_), channel_id=1, source_target_pairs={{0,1},{1,0},{2,3},{3,2},{4,5},{5,4},{6,7},{7,6},{8,9},{9,8},{10,11... | collective-permute-start | bytes 483848 | tf_op jit(solution)/shard_map/ppermute | solution.py:35
  42.7 27.0 %collective-permute-start.13 = (bf16[480,496]{1,0:T(8,128)(2,1)S(1)}, bf16[480,496]{1,0:T(8,128)(2,1)S(1)}, u32[]{:S(2)}, u32[]{:S(2)}) collective-permute-start(bf16[480,496]{1,0:T(8,128)(2,1)S(1)} %bitcast.202), channel_id=1, source_target_pairs={{0,16},{1,17},{2,18},{3,19},{4,20},{5,21},{6,22},{7,23},{8,24},{9,... | collective-permute-start | bytes 1428488 | tf_op jit(solution)/shard_map/ppermute | solution.py:35
  46.1 24.1 %collective-permute-start.15 = (bf16[480,496]{1,0:T(8,128)(2,1)S(1)}, bf16[480,496]{1,0:T(8,128)(2,1)S(1)}, u32[]{:S(2)}, u32[]{:S(2)}) collective-permute-start(bf16[480,496]{1,0:T(8,128)(2,1)S(1)} %collective-permute-done.14.refs_2_.refs_10_.refs_13_), channel_id=1, source_target_pairs={{0,16},{1,17},{2,18},{3,19},{4,20},{5,21},{6,22},{7,23},{8,24},{9,... | collective-permute-start | bytes 1428488 | tf_op jit(solution)/shard_map/ppermute | solution.py:35
  52.1 18.3 %collective-permute-start.16 = (bf16[480,496]{1,0:T(8,128)(2,1)S(1)}, bf16[480,496]{1,0:T(8,128)(2,1)S(1)}, u32[]{:S(2)}, u32[]{:S(2)}) collective-permute-start(bf16[480,496]{1,0:T(8,128)(2,1)S(1)} %bitcast.203), channel_id=1, source_target_pairs={{0,8},{1,9},{2,10},{3,11},{4,12},{5,13},{6,14},{7,15},{8,0},{9,1},... | collective-permute-start | bytes 1428488 | tf_op jit(solution)/shard_map/ppermute | solution.py:35
  77.4 24.2 %collective-permute-start.37 = (bf16[240,960]{1,0:T(8,128)(2,1)S(1)}, bf16[240,960]{1,0:T(8,128)(2,1)S(1)}, u32[]{:S(2)}, u32[]{:S(2)}) collective-permute-start(bf16[240,960]{1,0:T(8,128)(2,1)S(1)} %pad_maximum_fusion.1.refs_8_.refs_0_), channel_id=1, source_target_pairs={{0,2},{1,3},{2,4},{3,5},{4,6},{5,7},{6,0},{7,1},{8,10},{9,11},{10,... | collective-permute-start | bytes 1382408 | tf_op jit(solution)/shard_map/ppermute | solution.py:35
  80.4 22.3 %collective-permute-start.36 = (bf16[240,960]{1,0:T(8,128)(2,1)S(1)}, bf16[240,960]{1,0:T(8,128)(2,1)S(1)}, u32[]{:S(2)}, u32[]{:S(2)}) collective-permute-start(bf16[240,960]{1,0:T(8,128)(2,1)S(1)} %pad_maximum_fusion.1.refs_8_.refs_0_), channel_id=1, source_target_pairs={{0,6},{1,7},{2,0},{3,1},{4,2},{5,3},{6,4},{7,5},{8,14},{9,15},{10,... | collective-permute-start | bytes 1382408 | tf_op jit(solution)/shard_map/ppermute | solution.py:35
  102.7 16.9 %collective-permute-start.38 = (bf16[240,960]{1,0:T(8,128)(2,1)S(1)}, bf16[240,960]{1,0:T(8,128)(2,1)S(1)}, u32[]{:S(2)}, u32[]{:S(2)}) collective-permute-start(bf16[240,960]{1,0:T(8,128)(2,1)S(1)} %collective-permute-done.36.refs_9_.refs_1_), channel_id=1, source_target_pairs={{0,6},{1,7},{2,0},{3,1},{4,2},{5,3},{6,4},{7,5},{8,14},{9,15},{10,... | collective-permute-start | bytes 1382408 | tf_op jit(solution)/shard_map/ppermute | solution.py:35
  103.7 15.9 %collective-permute-start.42 = (bf16[960,128]{1,0:T(8,128)(2,1)}, bf16[960,128]{1,0:T(8,128)(2,1)S(1)}, u32[]{:S(2)}, u32[]{:S(2)}) collective-permute-start(bf16[960,128]{1,0:T(8,128)(2,1)} %bitcast.237), channel_id=1, source_target_pairs={{0,8},{1,9},{2,10},{3,11},{4,12},{5,13},{6,14},{7,15},{8,0},{9,1},... | collective-permute-start | bytes 737288 | tf_op jit(solution)/shard_map/ppermute | solution.py:35
  129.5 36.4 %collective-permute-start.50 = (bf16[4,4,240,128]{3,2,1,0:T(8,128)(2,1)}, bf16[4,4,240,128]{3,2,1,0:T(8,128)(2,1)S(1)}, u32[]{:S(2)}, u32[]{:S(2)}) collective-permute-start(bf16[4,4,240,128]{3,2,1,0:T(8,128)(2,1)} %get-tuple-element.73), channel_id=1, source_target_pairs={{0,8},{1,9},{2,10},{3,11},{4,12},{5,13},{6,14},{7,15},{8,0},{9,1},... | collective-permute-start | bytes 2949128 | tf_op jit(solution)/shard_map/ppermute | solution.py:35
  136.0 24.3 %collective-permute-start.76 = (bf16[240,960]{1,0:T(8,128)(2,1)}, bf16[240,960]{1,0:T(8,128)(2,1)S(1)}, u32[]{:S(2)}, u32[]{:S(2)}) collective-permute-start(bf16[240,960]{1,0:T(8,128)(2,1)} %get-tuple-element.98), channel_id=1, source_target_pairs={{0,6},{1,7},{2,0},{3,1},{4,2},{5,3},{6,4},{7,5},{8,14},{9,15},{10,... | collective-permute-start | bytes 1382408 | tf_op jit(solution)/shard_map/ppermute | solution.py:35
  136.1 33.3 %collective-permute-start.75 = (bf16[240,960]{1,0:T(8,128)(2,1)}, bf16[240,960]{1,0:T(8,128)(2,1)S(1)}, u32[]{:S(2)}, u32[]{:S(2)}) collective-permute-start(bf16[240,960]{1,0:T(8,128)(2,1)} %get-tuple-element.96), channel_id=1, source_target_pairs={{0,2},{1,3},{2,4},{3,5},{4,6},{5,7},{6,0},{7,1},{8,10},{9,11},{10,... | collective-permute-start | bytes 1382408 | tf_op jit(solution)/shard_map/ppermute | solution.py:35
  166.0 28.3 %collective-permute-start.46 = (bf16[4,4,240,128]{3,2,1,0:T(8,128)(2,1)}, bf16[4,4,240,128]{3,2,1,0:T(8,128)(2,1)S(1)}, u32[]{:S(2)}, u32[]{:S(2)}) collective-permute-start(bf16[4,4,240,128]{3,2,1,0:T(8,128)(2,1)} %get-tuple-element.67), channel_id=1, source_target_pairs={{0,8},{1,9},{2,10},{3,11},{4,12},{5,13},{6,14},{7,15},{8,0},{9,1},... | collective-permute-start | bytes 2949128 | tf_op jit(solution)/shard_map/ppermute | solution.py:35
  174.8 36.4 %collective-permute-start.78 = (bf16[120,640]{1,0:T(8,128)(2,1)S(1)}, bf16[120,640]{1,0:T(8,128)(2,1)S(1)}, u32[]{:S(2)}, u32[]{:S(2)}) collective-permute-start(bf16[120,640]{1,0:T(8,128)(2,1)S(1)} %select_convert_fusion), channel_id=1, source_target_pairs={{0,1},{1,0},{2,3},{3,2},{4,5},{5,4},{6,7},{7,6},{8,9},{9,8},{10,11... | collective-permute-start | bytes 460808 | tf_op jit(solution)/shard_map/ppermute | solution.py:35
  195.3 19.4 %collective-permute-start.54 = (bf16[640,128]{1,0:T(8,128)(2,1)S(1)}, bf16[640,128]{1,0:T(8,128)(2,1)S(1)}, u32[]{:S(2)}, u32[]{:S(2)}) collective-permute-start(bf16[640,128]{1,0:T(8,128)(2,1)S(1)} %copy-done.61), channel_id=1, source_target_pairs={{0,1},{1,0},{2,3},{3,2},{4,5},{5,4},{6,7},{7,6},{8,9},{9,8},{10,11... | collective-permute-start | bytes 491528 | tf_op jit(solution)/shard_map/ppermute | solution.py:35
  204.5 54.0 %collective-permute-start.68 = (bf16[4,480,496]{2,1,0:T(8,128)(2,1)}, bf16[4,480,496]{2,1,0:T(8,128)(2,1)}, u32[]{:S(2)}, u32[]{:S(2)}) collective-permute-start(bf16[4,480,496]{2,1,0:T(8,128)(2,1)} %get-tuple-element.92), channel_id=1, source_target_pairs={{0,8},{1,9},{2,10},{3,11},{4,12},{5,13},{6,14},{7,15},{8,0},{9,1},... | collective-permute-start | bytes 5713928 | tf_op jit(solution)/shard_map/ppermute | solution.py:35
  210.1 15.7 %collective-permute-start.58 = (bf16[640,128]{1,0:T(8,128)(2,1)S(1)}, bf16[640,128]{1,0:T(8,128)(2,1)S(1)}, u32[]{:S(2)}, u32[]{:S(2)}) collective-permute-start(bf16[640,128]{1,0:T(8,128)(2,1)S(1)} %add_convert_fusion.14), channel_id=1, source_target_pairs={{0,4},{1,5},{2,6},{3,7},{4,0},{5,1},{6,2},{7,3},{8,12},{9,13},{10,... | collective-permute-start | bytes 491528 | tf_op jit(solution)/shard_map/ppermute | solution.py:35
  214.7 16.8 %collective-permute-start.79 = (bf16[240,320]{1,0:T(8,128)(2,1)S(1)}, bf16[240,320]{1,0:T(8,128)(2,1)S(1)}, u32[]{:S(2)}, u32[]{:S(2)}) collective-permute-start(bf16[240,320]{1,0:T(8,128)(2,1)S(1)} %slice.600), channel_id=1, source_target_pairs={{0,0},{1,1},{2,8},{3,9},{4,16},{5,17},{6,24},{7,25},{8,2},{9,3},{1... | collective-permute-start | bytes 460808 | tf_op jit(solution)/shard_map/ppermute | solution.py:35
  215.6 45.0 %collective-permute-start.47 = (bf16[4,240,128]{2,1,0:T(8,128)(2,1)}, bf16[4,240,128]{2,1,0:T(8,128)(2,1)}, u32[]{:S(2)}, u32[]{:S(2)}) collective-permute-start(bf16[4,240,128]{2,1,0:T(8,128)(2,1)} %get-tuple-element.132), channel_id=1, source_target_pairs={{0,16},{1,17},{2,18},{3,19},{4,20},{5,21},{6,22},{7,23},{8,24},{9,... | collective-permute-start | bytes 737288 | tf_op jit(solution)/shard_map/ppermute | solution.py:35
  235.8 16.2 %collective-permute-start.63 = (bf16[4,168,120]{2,1,0:T(8,128)(2,1)}, bf16[4,168,120]{2,1,0:T(8,128)(2,1)}, u32[]{:S(2)}, u32[]{:S(2)}) collective-permute-start(bf16[4,168,120]{2,1,0:T(8,128)(2,1)} %get-tuple-element.137), channel_id=1, source_target_pairs={{0,1},{1,0},{2,3},{3,2},{4,5},{5,4},{6,7},{7,6},{8,9},{9,8},{10,11... | collective-permute-start | bytes 483848 | tf_op jit(solution)/shard_map/ppermute | solution.py:35
  242.0 20.2 %collective-permute-start.49 = (bf16[4,240,128]{2,1,0:T(8,128)(2,1)S(1)}, bf16[4,240,128]{2,1,0:T(8,128)(2,1)S(1)}, u32[]{:S(2)}, u32[]{:S(2)}) collective-permute-start(bf16[4,240,128]{2,1,0:T(8,128)(2,1)S(1)} %get-tuple-element.133), channel_id=1, source_target_pairs={{0,17},{1,16},{2,19},{3,18},{4,21},{5,20},{6,23},{7,22},{8,25},{9,... | collective-permute-start | bytes 737288 | tf_op jit(solution)/shard_map/ppermute | solution.py:35
  244.2 18.9 %collective-permute-start.48 = (bf16[4,240,128]{2,1,0:T(8,128)(2,1)S(1)}, bf16[4,240,128]{2,1,0:T(8,128)(2,1)S(1)}, u32[]{:S(2)}, u32[]{:S(2)}) collective-permute-start(bf16[4,240,128]{2,1,0:T(8,128)(2,1)S(1)} %get-tuple-element.134), channel_id=1, source_target_pairs={{0,1},{1,0},{2,3},{3,2},{4,5},{5,4},{6,7},{7,6},{8,9},{9,8},{10,11... | collective-permute-start | bytes 737288 | tf_op jit(solution)/shard_map/ppermute | solution.py:35
  263.1 19.4 %collective-permute-start.71 = (bf16[480,496]{1,0:T(8,128)(2,1)S(1)}, bf16[480,496]{1,0:T(8,128)(2,1)S(1)}, u32[]{:S(2)}, u32[]{:S(2)}) collective-permute-start(bf16[480,496]{1,0:T(8,128)(2,1)S(1)} %get-tuple-element.122), channel_id=1, source_target_pairs={{0,17},{1,16},{2,19},{3,18},{4,21},{5,20},{6,23},{7,22},{8,25},{9,... | collective-permute-start | bytes 1428488 | tf_op jit(solution)/shard_map/ppermute | solution.py:35
  264.7 19.1 %collective-permute-start.70 = (bf16[480,496]{1,0:T(8,128)(2,1)S(1)}, bf16[480,496]{1,0:T(8,128)(2,1)S(1)}, u32[]{:S(2)}, u32[]{:S(2)}) collective-permute-start(bf16[480,496]{1,0:T(8,128)(2,1)S(1)} %get-tuple-element.123), channel_id=1, source_target_pairs={{0,1},{1,0},{2,3},{3,2},{4,5},{5,4},{6,7},{7,6},{8,9},{9,8},{10,11... | collective-permute-start | bytes 1428488 | tf_op jit(solution)/shard_map/ppermute | solution.py:35
  (120 other events, 1459.9 us)
